TPU v7x, 32 devices: a whole 2x2x4 slice. The times are simulated.
32 devices in a mesh: grp: 4 (over y, core), ctx: 2 (over x), tp: 4 (over z).
Axes of the slice: x: 2, y: 2, z: 4, core: 2. Of those that a mesh axis runs over, the one named last changes fastest.
Arguments:
- state: float32 [4, 32, 5120], P(None, 'ctx', ('grp', 'tp')), may hold values from -6 to 6
- clean_tokens: bfloat16 [32, 5120], P('ctx', ('grp', 'tp')), may hold values from -6 to 6
- w_query: bfloat16 [5120, 4096], P('ctx', ('grp', 'tp')), may hold values from -0.078125 to 0.078125
- w_key: bfloat16 [5120, 4096], P('ctx', ('grp', 'tp')), may hold values from -0.078125 to 0.078125
- w_value: bfloat16 [5120, 4096], P('ctx', ('grp', 'tp')), may hold values from -0.078125 to 0.078125
- w_out: bfloat16 [4096, 5120], P(('grp', 'tp'), 'ctx'), may hold values from -0.09375 to 0.09375
- cache_keys: bfloat16 [1024, 4096], P('ctx', ('grp', 'tp')), may hold values from -200 to 200
- cache_values: bfloat16 [1024, 4096], P('ctx', ('grp', 'tp')), may hold values from -6 to 6
- norm_gain: float32 [5120], P(('grp', 'tp')), may hold values from 0.25 to 1.75
- mod_gain: float32 [5120], P(('grp', 'tp')), may hold values from -3 to 3
- out_gain: float32 [5120], P(('grp', 'tp')), may hold values from 0.1 to 1.9
- levels: float32 [50], replicated, may hold values from 0.05 to 1
- noise_index: int32 [4], replicated, may hold values from 0 to 47
- placement: int32 [4], P('ctx'), may hold values from 0 to 3, each once
- group_mask: int32 [4, 4], replicated, may hold values 0 or 1
Outputs:
- new_state: float32 [4, 32, 5120], P(None, 'ctx', ('grp', 'tp'))
- new_keys: bfloat16 [32, 4096], P('ctx', ('grp', 'tp'))
- new_values: bfloat16 [32, 4096], P('ctx', ('grp', 'tp'))
All inputs are finite; a program needn't handle non-finite values.
Results may differ from a plain program's by a relative error of at most 0.0062.
The roundings to bfloat16 on the way count: a program that leaves them out, or rounds other values in their place, can miss the bound.
Values may be sent and summed in bfloat16 or wider, within the bound.
A program may use at most 64 MiB of HBM per device.

v0:
```python
import functools
import math

import jax
import jax.numpy as jnp
from jax import lax
from jax.experimental import pallas as pl
from jax.experimental.pallas import tpu as pltpu
from jax.sharding import PartitionSpec as P

D = 5120
HD = 128
SLOT = 256


epsilon = 1e-06


def level_lookup(levels, indices):
    table = jnp.arange(levels.shape[0], dtype=jnp.int32)
    picked = (indices[:, None] == table[None, :]).astype(jnp.float32)
    return jnp.sum(picked * levels[None, :], axis=1)


def normalize_rows(rows, sigma_rows, norm_gain, mod_gain):
    squares = lax.psum(jnp.sum(rows * rows, axis=1), ("grp", "tp"))
    inverse = lax.rsqrt(squares / D + epsilon)
    scaled = (
        rows
        * inverse[:, None]
        * norm_gain[None, :]
        * (1.0 + sigma_rows[:, None] * mod_gain[None, :])
    )
    return lax.all_gather(scaled.astype(jnp.bfloat16), ("grp", "tp"), axis=1, tiled=True)


def local(
    state,
    clean_tokens,
    w_query,
    w_key,
    w_value,
    w_out,
    cache_keys,
    cache_values,
    norm_gain,
    mod_gain,
    out_gain,
    levels,
    noise_index,
    placement,
    group_mask,
):
    flight, ch_dev, local_width = state.shape
    ctx_count = lax.axis_size("ctx")
    group = ch_dev * ctx_count
    cache_dev = cache_keys.shape[0]
    slots_dev = cache_dev // SLOT
    heads_dev = cache_keys.shape[1] // HD
    rows_count = flight * ch_dev
    scale = 1.0 / math.sqrt(HD)
    wk_full, wv_full, wo_full = (
        lax.all_gather(w_key, "ctx", axis=0, tiled=True),
        lax.all_gather(w_value, "ctx", axis=0, tiled=True),
        lax.all_gather(w_out, "ctx", axis=1, tiled=True),
    )
    group_table = jnp.arange(group_mask.shape[1], dtype=jnp.int32)
    slot_onehot = (placement[:, None] == group_table[None, :]).astype(jnp.int32)
    slot_seen = jnp.sum(slot_onehot[None, :, :] * group_mask[:, None, :], axis=2) > 0
    cache_seen = slot_seen[:, None, None, :, None]
    own_group = jnp.arange(flight, dtype=jnp.int32)
    flight_seen = (own_group[None, :] <= own_group[:, None])[:, None, None, :, None]
    cache_k = cache_keys.reshape(slots_dev, SLOT, heads_dev, HD)
    cache_v = cache_values.reshape(slots_dev, SLOT, heads_dev, HD)
    finished_keys = None
    finished_values = None
    current = level_lookup(levels, noise_index + 0)
    following = level_lookup(levels, noise_index + 0 + 1)
    rows = state.reshape(rows_count, local_width)
    sigma_rows = jnp.repeat(current, ch_dev)
    rows = jnp.concatenate([rows, clean_tokens.astype(jnp.float32)], axis=0)
    sigma_rows = jnp.concatenate([sigma_rows, jnp.zeros((ch_dev,), jnp.float32)])
    features = normalize_rows(rows, sigma_rows, norm_gain, mod_gain)
    keys_new = jnp.dot(features, wk_full, preferred_element_type=jnp.float32).astype(jnp.bfloat16)
    values_new = jnp.dot(features, wv_full, preferred_element_type=jnp.float32).astype(jnp.bfloat16)
    finished_keys = keys_new[rows_count:]
    finished_values = values_new[rows_count:]
    keys_new = keys_new[:rows_count]
    values_new = values_new[:rows_count]
    noisy = features[:rows_count]
    pieces = lax.all_to_all(
        noisy.reshape(flight, ch_dev, -1), "ctx", split_axis=2, concat_axis=1, tiled=True
    )
    partial_q = jnp.einsum("fqd,de->fqe", pieces, w_query, preferred_element_type=jnp.float32)
    queries = lax.psum(partial_q, "ctx").astype(jnp.bfloat16)
    query_heads = queries.reshape(flight, group, heads_dev, HD)
    finished_k = finished_keys.reshape(ch_dev, heads_dev, HD)
    finished_v = finished_values.reshape(ch_dev, heads_dev, HD)
    flight_k = keys_new.reshape(flight, ch_dev, heads_dev, HD)
    flight_v = values_new.reshape(flight, ch_dev, heads_dev, HD)
    cache_scores = (
        jnp.einsum("fqhd,sthd->fqhst", query_heads, cache_k, preferred_element_type=jnp.float32)
        * scale
    )
    finished_scores = (
        jnp.einsum("fqhd,thd->fqht", query_heads, finished_k, preferred_element_type=jnp.float32)
        * scale
    )
    flight_scores = (
        jnp.einsum("fqhd,gthd->fqhgt", query_heads, flight_k, preferred_element_type=jnp.float32)
        * scale
    )
    peak = jnp.max(finished_scores, axis=3)
    peak = jnp.maximum(peak, jnp.max(jnp.where(cache_seen, cache_scores, -jnp.inf), axis=(3, 4)))
    peak = jnp.maximum(peak, jnp.max(jnp.where(flight_seen, flight_scores, -jnp.inf), axis=(3, 4)))
    peak = lax.pmax(peak, "ctx")
    cache_p = jnp.where(cache_seen, jnp.exp(cache_scores - peak[..., None, None]), 0.0).astype(
        jnp.bfloat16
    )
    finished_p = jnp.exp(finished_scores - peak[..., None]).astype(jnp.bfloat16)
    flight_p = jnp.where(flight_seen, jnp.exp(flight_scores - peak[..., None, None]), 0.0).astype(
        jnp.bfloat16
    )
    numer = jnp.einsum("fqhst,sthd->fqhd", cache_p, cache_v, preferred_element_type=jnp.float32)
    numer = numer + jnp.einsum(
        "fqht,thd->fqhd", finished_p, finished_v, preferred_element_type=jnp.float32
    )
    numer = numer + jnp.einsum(
        "fqhgt,gthd->fqhd", flight_p, flight_v, preferred_element_type=jnp.float32
    )
    denom = jnp.sum(cache_p, axis=(3, 4), dtype=jnp.float32)
    denom = denom + jnp.sum(finished_p, axis=3, dtype=jnp.float32)
    denom = denom + jnp.sum(flight_p, axis=(3, 4), dtype=jnp.float32)
    numer, denom = (
        lax.psum_scatter(
            numer.reshape(flight, group, heads_dev * HD), "ctx", scatter_dimension=1, tiled=True
        ),
        lax.psum_scatter(denom, "ctx", scatter_dimension=1, tiled=True),
    )
    attention = numer.reshape(flight, ch_dev, heads_dev, HD) / denom[..., None]
    attention = attention.astype(jnp.bfloat16).reshape(rows_count, heads_dev * HD)
    partial_y = jnp.dot(attention, wo_full, preferred_element_type=jnp.float32)
    y_rows = lax.psum_scatter(partial_y, ("grp", "tp"), scatter_dimension=1, tiled=True)
    y_squares = lax.psum(jnp.sum(y_rows * y_rows, axis=1), ("grp", "tp"))
    velocity = y_rows * lax.rsqrt(y_squares / D + epsilon)[:, None] * out_gain[None, :]
    state = state + (following - current)[:, None, None] * velocity.reshape(
        flight, ch_dev, local_width
    )
    return (state, finished_keys, finished_values)


MESH = pl.DeviceIdType.MESH


def remote(src, dst, send, recv, device):
    return pltpu.make_async_remote_copy(
        src_ref=src,
        dst_ref=dst,
        send_sem=send,
        recv_sem=recv,
        device_id=device,
        device_id_type=MESH,
    )


def row_squares(rows, lanes):
    squares = rows * rows
    count = squares.shape[0]
    if count < lanes:
        squares = jnp.concatenate(
            [squares, jnp.zeros((lanes - count, squares.shape[1]), jnp.float32)], axis=0
        )
    ones = jnp.ones((8, squares.shape[1]), jnp.float32)
    return lax.dot_general(
        ones,
        squares,
        (((1,), (1,)), ((), ())),
        precision=lax.Precision.HIGHEST,
        preferred_element_type=jnp.float32,
    )


def kernel(
    dims,
    state_hbm,
    clean_hbm,
    wq_hbm,
    wk_hbm,
    wv_hbm,
    wo_hbm,
    ck_hbm,
    cv_hbm,
    ng_hbm,
    mg_hbm,
    og_hbm,
    levels_hbm,
    noise_hbm,
    place_hbm,
    mask_hbm,
    out_ref,
    nk_ref,
    nv_ref,
    state_ref,
    clean_ref,
    ng_ref,
    mg_ref,
    og_ref,
    levels_ref,
    noise_ref,
    place_ref,
    mask_ref,
    w_buf,
    wo_buf,
    cache_buf,
    seen_buf,
    ssq_buf,
    ssy_buf,
    h_own,
    h_buf,
    acc,
    part,
    part_in,
    kv_buf,
    fin_in,
    att_buf,
    y_part,
    y_send,
    y_in1,
    v_send,
    v_in,
    z_send,
    z_in,
    local_sem,
    cache_s,
    cache_r,
    ssq_s,
    ssq_r,
    a_s,
    a_r,
    b_s,
    b_r,
    n_s,
    n_r,
    c_s,
    c_r,
    p_s,
    p_r,
    f_s,
    f_r,
    t_s,
    t_r,
    y1_s,
    y1_r,
    yv_s,
    yv_r,
    y2_s,
    y2_r,
    ssy_s,
    ssy_r,
):
    n_grp, n_ctx, n_tp = dims
    per = n_grp // n_ctx
    members = n_grp * n_tp
    flight, ch, width = state_hbm.shape
    rows_count = flight * ch
    all_rows = rows_count + ch
    cache_dev = ck_hbm.shape[0]
    lanes = ssq_buf.shape[2]
    total_rows = n_ctx * all_rows
    g, c, t = lax.axis_index("grp"), lax.axis_index("ctx"), lax.axis_index("tp")
    u, k = g // per, g % per
    j = g * n_tp + t
    other = 1 - c
    partner = (g, other, t)
    sibling = (u * per + (1 - k), c, t)
    beside = ((1 - u) * per + k, c, t)
    held = 1 - u
    at_home = u == c
    cross = ((1 - u) * per + k, other, t)

    def member(index):
        return (index // n_tp, c, index % n_tp)

    def zpeer(d):
        return (g, c, (t + d) % n_tp)

    loads = [
        pltpu.make_async_copy(wq_hbm, w_buf.at[0], local_sem.at[0]),
        pltpu.make_async_copy(wk_hbm, w_buf.at[1], local_sem.at[1]),
        pltpu.make_async_copy(wv_hbm, w_buf.at[2], local_sem.at[2]),
        pltpu.make_async_copy(wo_hbm, wo_buf, local_sem.at[3]),
    ]
    own_lanes = pl.ds(pl.multiple_of(c * HD, HD), HD)
    other_lanes = pl.ds(pl.multiple_of(other * HD, HD), HD)
    cache_loads = [
        pltpu.make_async_copy(ck_hbm.at[:, own_lanes], cache_buf.at[0, c], local_sem.at[4]),
        pltpu.make_async_copy(cv_hbm.at[:, own_lanes], cache_buf.at[1, c], local_sem.at[5]),
    ]
    small = [
        pltpu.make_async_copy(src, dst, local_sem.at[6 + i])
        for i, (src, dst) in enumerate(
            [
                (state_hbm, state_ref),
                (clean_hbm, clean_ref),
                (ng_hbm, ng_ref),
                (mg_hbm, mg_ref),
                (og_hbm, og_ref),
                (levels_hbm, levels_ref),
                (noise_hbm, noise_ref),
                (place_hbm, place_ref),
                (mask_hbm, mask_ref),
            ]
        )
    ]
    for copy in small + loads + cache_loads:
        copy.start()

    barrier = pltpu.get_barrier_semaphore()
    for d in range(1, members):
        pl.semaphore_signal(barrier, inc=1, device_id=member((j + d) % members), device_id_type=MESH)
    pl.semaphore_signal(barrier, inc=1, device_id=partner, device_id_type=MESH)
    pl.semaphore_signal(barrier, inc=1, device_id=cross, device_id_type=MESH)
    for copy in small:
        copy.wait()

    rows = jnp.concatenate(
        [state_ref[...].reshape(rows_count, width), clean_ref[...].astype(jnp.float32)], axis=0
    )
    ssq_buf[0] = row_squares(rows, lanes)[0:1]
    line = lax.broadcasted_iota(jnp.int32, (8, SLOT), 0)
    for s in range(cache_dev // SLOT):
        block = jnp.zeros((8, SLOT), jnp.float32)
        for f in range(flight):
            shown = jnp.where(mask_ref[f, place_ref[s]] != 0, 1.0, 0.0)
            block = jnp.where(line == f, shown, block)
        seen_buf[c, :, s * SLOT : (s + 1) * SLOT] = block
    pl.semaphore_wait(barrier, members + 1)

    def exchange(buf, send, recv):
        copies = [
            remote(
                buf.at[0], buf.at[d], send.at[d - 1], recv.at[d - 1], member((j + d) % members)
            )
            for d in range(1, members)
        ]
        for copy in copies:
            copy.start()
        return copies

    ssq_copies = exchange(ssq_buf, ssq_s, ssq_r)
    cache_copies = [
        remote(seen_buf.at[c], seen_buf.at[c], cache_s.at[0], cache_r.at[0], partner),
        remote(
            ck_hbm.at[:, other_lanes], cache_buf.at[0, c], cache_s.at[1], cache_r.at[1], partner
        ),
        remote(
            cv_hbm.at[:, other_lanes], cache_buf.at[1, c], cache_s.at[2], cache_r.at[2], partner
        ),
    ]
    for copy in cache_copies[:2]:
        copy.start()
    for copy in ssq_copies:
        copy.wait_recv()

    total = ssq_buf[0]
    for d in range(1, members):
        total = total + ssq_buf[d]
    inverse = lax.rsqrt(jnp.transpose(jnp.broadcast_to(total, (8, lanes)))[:all_rows, 0:1] / D + epsilon)
    modulation = mg_ref[...].reshape(1, width)
    scaled = rows * inverse * ng_ref[...].reshape(1, width)
    blocks = []
    for f in range(flight):
        sigma = levels_ref[noise_ref[f]]
        blocks.append(scaled[f * ch : (f + 1) * ch] * (1.0 + sigma * modulation))
    blocks.append(scaled[rows_count:])
    features = jnp.concatenate(blocks, axis=0).astype(jnp.bfloat16)
    h_own[...] = features

    mine = k * n_tp + t
    a_copy = remote(
        h_own, h_buf.at[mine, c], a_s.at[0], a_r.at[0], ((1 - c) * per + k, u, t)
    )
    a_copy.start()
    cache_copies[2].start()
    remote(h_own, h_buf.at[mine, held], a_s.at[0], a_r.at[0], partner).wait_recv()

    stage_b = []

    def forward(x, index, send, recv, where, device):
        copy = remote(h_buf.at[index, x], h_buf.at[index, x], send.at[where], recv.at[where], device)
        copy.start()
        stage_b.append(copy)

    def arrived(x, index, send, recv, where, device):
        remote(
            h_buf.at[index, x], h_buf.at[index, x], send.at[where], recv.at[where], device
        ).wait_recv()

    def slot_of(core, d):
        return core * n_tp + (t + n_tp - d) % n_tp

    for d in range(1, n_tp):
        forward(held, mine, b_s, b_r, d - 1, zpeer(d))
    forward(held, mine, n_s, n_r, 0, beside)
    forward(held, mine, c_s, c_r, 0, sibling)
    for d in range(1, n_tp):
        arrived(held, slot_of(k, d), b_s, b_r, d - 1, zpeer(d))
        forward(held, slot_of(k, d), n_s, n_r, d, beside)
        forward(held, slot_of(k, d), c_s, c_r, d, sibling)

    for copy in loads[:3]:
        copy.wait()

    def project(slot, i):
        lhs = h_buf[slot].reshape(total_rows, width)
        depth = pl.ds(pl.multiple_of(slot * width, 64), width)
        return jnp.dot(lhs, w_buf[i, depth, :], preferred_element_type=jnp.float32)

    for d in range(n_tp):
        slot = slot_of(k, d)
        arrived(u, slot, n_s, n_r, d, beside)
        forward(u, slot, c_s, c_r, n_tp + d, sibling)
        for i in range(3):
            acc[i] = project(slot, i) if d == 0 else acc[i] + project(slot, i)
    part_copies = []
    for d in range(n_tp):
        slot = slot_of(1 - k, d)
        arrived(held, slot, c_s, c_r, d, sibling)
        arrived(u, slot, c_s, c_r, n_tp + d, sibling)
        for i in range(3):
            if d < n_tp - 1:
                acc[i] = acc[i] + project(slot, i)
                continue
            whole = acc[i] + project(slot, i)
            for head in range(n_ctx):
                part[head, i] = whole[:, head * HD : (head + 1) * HD]
            copy = remote(part.at[other, i], part_in.at[i], p_s.at[i], p_r.at[i], partner)
            copy.start()
            part_copies.append(copy)
    for copy in cache_loads:
        copy.wait()
    for i, copy in enumerate(cache_copies):
        copy.wait_recv()
    row_group = (lax.broadcasted_iota(jnp.int32, (total_rows, 8), 0) % all_rows) // ch
    pick = (row_group == lax.broadcasted_iota(jnp.int32, (total_rows, 8), 1)).astype(jnp.bfloat16)
    seen = [
        jnp.dot(pick, seen_buf[x].astype(jnp.bfloat16), preferred_element_type=jnp.float32) > 0.5
        for x in range(n_ctx)
    ]
    query_group = (lax.broadcasted_iota(jnp.int32, (total_rows, total_rows), 0) % all_rows) // ch
    key_group = (lax.broadcasted_iota(jnp.int32, (total_rows, total_rows), 1) % all_rows) // ch
    seen.append(jnp.logical_or(key_group == flight, key_group <= query_group))

    part_copies[0].wait_recv()
    q = (part[c, 0] + part_in[0]).astype(jnp.bfloat16)
    scale = 1.0 / math.sqrt(HD)

    def score(keys):
        return (
            lax.dot_general(q, keys, (((1,), (1,)), ((), ())), preferred_element_type=jnp.float32)
            * scale
        )

    scores = [score(cache_buf[0, x]) for x in range(n_ctx)]
    part_copies[1].wait_recv()
    key = (part[c, 1] + part_in[1]).astype(jnp.bfloat16)
    scores.append(score(key))
    scores = [jnp.where(s, v, -jnp.inf) for s, v in zip(seen, scores)]
    peak = functools.reduce(
        jnp.maximum, [jnp.max(v, axis=1, keepdims=True) for v in scores]
    )
    weights = [
        jnp.where(s, jnp.exp(v - peak), 0.0).astype(jnp.bfloat16) for s, v in zip(seen, scores)
    ]
    denom = sum(jnp.sum(w.astype(jnp.float32), axis=1, keepdims=True) for w in weights)
    part_copies[2].wait_recv()
    value = (part[c, 2] + part_in[2]).astype(jnp.bfloat16)
    values = [cache_buf[1, x] for x in range(n_ctx)] + [value]
    numer = sum(
        jnp.dot(w, v, preferred_element_type=jnp.float32) for w, v in zip(weights, values)
    )
    attention = (numer / denom).astype(jnp.bfloat16)
    for x in range(n_ctx):
        att_buf[c, x * rows_count : (x + 1) * rows_count, :] = attention[
            x * all_rows : x * all_rows + rows_count
        ]
    att_copy = remote(att_buf.at[c], att_buf.at[c], t_s.at[0], t_r.at[0], partner)
    att_copy.start()

    for x in range(n_ctx):
        last = slice(x * all_rows + rows_count, (x + 1) * all_rows)
        kv_buf[x, 0] = key[last]
        kv_buf[x, 1] = value[last]
    fin_copy = remote(kv_buf.at[other], fin_in, f_s.at[0], f_r.at[0], partner)
    fin_copy.start()
    nk_ref[:, own_lanes] = kv_buf[c, 0]
    nv_ref[:, own_lanes] = kv_buf[c, 1]

    loads[3].wait()
    att_copy.wait_recv()
    both = jnp.concatenate([att_buf[x] for x in range(n_ctx)], axis=1)
    y1 = []
    for tt in range(n_tp):
        for kk in range(per):
            start = (kk * n_tp + tt) * width
            piece = jnp.dot(
                both, wo_buf[:, start : start + width], preferred_element_type=jnp.float32
            )
            for x in range(n_ctx):
                half = piece[x * rows_count : (x + 1) * rows_count]
                y_part[kk, tt, x] = half
                y_send[kk, tt, x] = half.astype(jnp.bfloat16)
        copy = remote(y_send.at[1 - k, tt], y_in1.at[tt], y1_s.at[tt], y1_r.at[tt], sibling)
        copy.start()
        y1.append(copy)
    yv = []
    near = []
    for d in range(1, n_tp + 1):
        tt = (t + d) % n_tp
        remote(
            y_send.at[1 - k, tt], y_in1.at[tt], y1_s.at[tt], y1_r.at[tt], sibling
        ).wait_recv()
        for i, x in enumerate((other, c)):
            v_send[i, d - 1] = (y_part[k, tt, x] + y_in1[tt, x].astype(jnp.float32)).astype(
                jnp.bfloat16
            )
            copy = remote(
                v_send.at[i, d - 1],
                v_in.at[u, d - 1],
                yv_s.at[i * n_tp + d - 1],
                yv_r.at[u * n_tp + d - 1],
                (c * per + k, other, t) if i == 0 else beside,
            )
            if i == 0:
                copy.start()
                yv.append(copy)
            else:
                near.append(copy)
                pl.when(jnp.logical_not(at_home))(copy.start)
    fin_copy.wait_recv()
    nk_ref[:, other_lanes] = fin_in[0]
    nv_ref[:, other_lanes] = fin_in[1]
    y2 = []
    for d in range(1, n_tp + 1):

        @pl.when(at_home)
        def _():
            v_in[u, d - 1] = v_send[1, d - 1]

        for y in range(n_ctx):

            @pl.when(jnp.logical_not(jnp.logical_and(at_home, u == y)))
            def _():
                remote(
                    v_send.at[0, d - 1],
                    v_in.at[y, d - 1],
                    yv_s.at[d - 1],
                    yv_r.at[y * n_tp + d - 1],
                    partner,
                ).wait_recv()

        summed = v_in[0, d - 1].astype(jnp.float32) + v_in[1, d - 1].astype(jnp.float32)
        if d < n_tp:
            z_send[d - 1] = summed.astype(jnp.bfloat16)
            copy = remote(
                z_send.at[d - 1], z_in.at[d - 1], y2_s.at[d - 1], y2_r.at[d - 1], zpeer(d)
            )
            copy.start()
            y2.append(copy)
    for d in range(1, n_tp):
        y2[d - 1].wait_recv()
        summed = summed + z_in[d - 1].astype(jnp.float32)
    y_rows = summed
    ssy_buf[0] = row_squares(y_rows, lanes)[0:1]
    ssy_copies = exchange(ssy_buf, ssy_s, ssy_r)
    for copy in ssq_copies + cache_copies + stage_b + part_copies + y1 + yv + y2:
        copy.wait_send()
    for copy in [a_copy, att_copy, fin_copy]:
        copy.wait_send()

    @pl.when(jnp.logical_not(at_home))
    def _():
        for copy in near:
            copy.wait_send()

    for copy in ssy_copies:
        copy.wait_recv()
    total = ssy_buf[0]
    for d in range(1, members):
        total = total + ssy_buf[d]
    inverse = lax.rsqrt(jnp.transpose(jnp.broadcast_to(total, (8, lanes)))[:rows_count, 0:1] / D + epsilon)
    velocity = y_rows * inverse * og_ref[...].reshape(1, width)
    for f in range(flight):
        now = levels_ref[noise_ref[f]]
        after = levels_ref[noise_ref[f] + 1]
        out_ref[f] = state_ref[f] + (after - now) * velocity[f * ch : (f + 1) * ch]
    for copy in ssy_copies:
        copy.wait_send()


def fused(dims, *args):
    state, clean_tokens, w_query = args[0], args[1], args[2]
    w_out, cache_keys = args[5], args[6]
    n_grp, n_ctx, n_tp = dims
    per = n_grp // n_ctx
    members = n_grp * n_tp
    flight, ch, width = state.shape
    rows_count = flight * ch
    all_rows = rows_count + ch
    total = n_ctx * all_rows
    lanes = -(-all_rows // 128) * 128
    queries = n_ctx * rows_count
    cache_dev = cache_keys.shape[0]
    bf, fl = jnp.bfloat16, jnp.float32
    dma = pltpu.SemaphoreType.DMA
    vm = pl.BlockSpec(memory_space=pltpu.VMEM)
    hbm = pl.BlockSpec(memory_space=pltpu.HBM)

    def pair(count):
        return [dma((count,))] * 2

    scratch = [
        pltpu.VMEM(state.shape, fl),
        pltpu.VMEM(clean_tokens.shape, bf),
        pltpu.VMEM((width,), fl),
        pltpu.VMEM((width,), fl),
        pltpu.VMEM((width,), fl),
        *[pltpu.SMEM(a.shape, a.dtype) for a in args[11:]],
        pltpu.VMEM((3,) + w_query.shape, bf),
        pltpu.VMEM(w_out.shape, bf),
        pltpu.VMEM((2, n_ctx, cache_dev, HD), bf),
        pltpu.VMEM((n_ctx, 8, cache_dev), fl),
        pltpu.VMEM((members, 1, lanes), fl),
        pltpu.VMEM((members, 1, lanes), fl),
        pltpu.VMEM((all_rows, width), bf),
        pltpu.VMEM((per * n_tp, n_ctx, all_rows, width), bf),
        pltpu.VMEM((3, total, n_ctx * HD), fl),
        pltpu.VMEM((n_ctx, 3, total, HD), fl),
        pltpu.VMEM((3, total, HD), fl),
        pltpu.VMEM((n_ctx, 2, ch, HD), bf),
        pltpu.VMEM((2, ch, HD), bf),
        pltpu.VMEM((n_ctx, queries, HD), bf),
        pltpu.VMEM((per, n_tp, n_ctx, rows_count, width), fl),
        pltpu.VMEM((per, n_tp, n_ctx, rows_count, width), bf),
        pltpu.VMEM((n_tp, n_ctx, rows_count, width), bf),
        pltpu.VMEM((n_ctx, n_tp, rows_count, width), bf),
        pltpu.VMEM((n_ctx, n_tp, rows_count, width), bf),
        pltpu.VMEM((n_tp - 1, rows_count, width), bf),
        pltpu.VMEM((n_tp - 1, rows_count, width), bf),
        dma((15,)),
        *pair(3),
        *pair(members - 1),
        *pair(1),
        *pair(n_tp - 1),
        *pair(n_tp),
        *pair(2 * n_tp),
        *pair(3),
        *pair(1),
        *pair(1),
        *pair(n_tp),
        *pair(n_ctx * n_tp),
        *pair(n_tp - 1),
        *pair(members - 1),
    ]
    return pl.pallas_call(
        functools.partial(kernel, dims),
        out_shape=(
            jax.ShapeDtypeStruct(state.shape, fl),
            jax.ShapeDtypeStruct((ch, cache_keys.shape[1]), bf),
            jax.ShapeDtypeStruct((ch, cache_keys.shape[1]), bf),
        ),
        in_specs=[hbm] * 15,
        out_specs=(vm, vm, vm),
        scratch_shapes=scratch,
        compiler_params=pltpu.CompilerParams(
            collective_id=0, has_side_effects=True, vmem_limit_bytes=67043328
        ),
    )(*args)


def step(dims, *args):
    n_grp, n_ctx, n_tp = dims
    heads_dev = args[6].shape[1] // HD
    if n_ctx == heads_dev == 2 and n_grp == 2 * n_ctx and args[0].shape[0] <= 8:
        return fused(dims, *args)
    return local(*args)


def solution(mesh):
    dims = tuple(mesh.shape[name] for name in ("grp", "ctx", "tp"))
    return jax.shard_map(
        functools.partial(step, dims),
        mesh=mesh,
        in_specs=(
            P(None, "ctx", ("grp", "tp")),
            P("ctx", ("grp", "tp")),
            P("ctx", ("grp", "tp")),
            P("ctx", ("grp", "tp")),
            P("ctx", ("grp", "tp")),
            P(("grp", "tp"), "ctx"),
            P("ctx", ("grp", "tp")),
            P("ctx", ("grp", "tp")),
            P(("grp", "tp")),
            P(("grp", "tp")),
            P(("grp", "tp")),
            P(),
            P(),
            P("ctx"),
            P(),
        ),
        out_specs=(P(None, "ctx", ("grp", "tp")), P("ctx", ("grp", "tp")), P("ctx", ("grp", "tp"))),
        check_vma=False,
    )
```

profile of v0, /device:TPU:0, one launch (start us, length us, event | category | flops | bytes accessed | tf_op | source)
XLA Modules:
  0.0 58.1 jit_solution(11138233601043275745)
XLA Ops:
  0.6 53.3 %shard_map.166 = (f32[4,16,320]{2,1,0:T(8,128)}, bf16[16,256]{1,0:T(8,128)(2,1)}, bf16[16,256]{1,0:T(8,128)(2,1)}) custom-call(f32[4,16,320]{2,1,0:T(8,128)} %state_hbm.1, bf16[16,320]{1,0:T(8,128)(2,1)} %clean_hbm.1, bf16[2560,256]{1,0:T(8,128)(2,1)} %wq_hbm.1, bf16[2560,256]{1,0:T(8,128)(2,1)} %wk_hbm.1, bf16[2560,256]{1,0:T(8,128)(2,1)} %wv_hbm.1, ...), custom_call_target="tpu_custom_call" | custom-call | tf_op jit(solution)/shard_map/pallas_call | solution.py:665
  53.9 1.5 %copy.21 = f32[4,16,320]{2,1,0:T(8,128)} copy(f32[4,16,320]{2,1,0:T(8,128)} %get-tuple-element.6) | data formatting | bytes 163840
  55.5 1.3 %copy.22 = bf16[16,256]{1,0:T(8,128)(2,1)} copy(bf16[16,256]{1,0:T(8,128)(2,1)} %get-tuple-element.7) | data formatting | bytes 16384
  56.8 1.3 %copy.23 = bf16[16,256]{1,0:T(8,128)(2,1)} copy(bf16[16,256]{1,0:T(8,128)(2,1)} %get-tuple-element.8) | data formatting | bytes 16384
where the time goes:
time: 58.3 us; the launch traced here: 58.1 us
  Pallas kernels  53.3 us (91%)
  local copies, waits for them, and re-layouts  4.13 us (7%)
  between operations  0.65 us (1%)
    pallas_call x1, Pallas kernels, fused(): pl.pallas_call(functools.partial(kernel, dims), out_shape=(jax.ShapeDtype...  53.3 us
    unnamed x3, local copies, waits for them, and re-layouts  4.13 us

commit v1 on v0

--- a/solution.py
+++ b/solution.py
@@ -150,6 +150,7 @@
 
 
 MESH = pl.DeviceIdType.MESH
+VMEM_LIMIT = 62 * 1024 * 1024
 
 
 def remote(src, dst, send, recv, device):
@@ -284,6 +285,12 @@
     def zpeer(d):
         return (g, c, (t + d) % n_tp)
 
+    barrier = pltpu.get_barrier_semaphore()
+    for d in range(1, members):
+        pl.semaphore_signal(barrier, inc=1, device_id=member((j + d) % members), device_id_type=MESH)
+    pl.semaphore_signal(barrier, inc=1, device_id=partner, device_id_type=MESH)
+    pl.semaphore_signal(barrier, inc=1, device_id=cross, device_id_type=MESH)
+
     loads = [
         pltpu.make_async_copy(wq_hbm, w_buf.at[0], local_sem.at[0]),
         pltpu.make_async_copy(wk_hbm, w_buf.at[1], local_sem.at[1]),
@@ -314,12 +321,6 @@
     ]
     for copy in small + loads + cache_loads:
         copy.start()
-
-    barrier = pltpu.get_barrier_semaphore()
-    for d in range(1, members):
-        pl.semaphore_signal(barrier, inc=1, device_id=member((j + d) % members), device_id_type=MESH)
-    pl.semaphore_signal(barrier, inc=1, device_id=partner, device_id_type=MESH)
-    pl.semaphore_signal(barrier, inc=1, device_id=cross, device_id_type=MESH)
     for copy in small:
         copy.wait()
 
@@ -598,6 +599,15 @@
         copy.wait_send()
 
 
+def write_out(*refs):
+    sems = refs[6]
+    copies = [pltpu.make_async_copy(refs[i], refs[3 + i], sems.at[i]) for i in range(3)]
+    for copy in copies:
+        copy.start()
+    for copy in copies:
+        copy.wait()
+
+
 def fused(dims, *args):
     state, clean_tokens, w_query = args[0], args[1], args[2]
     w_out, cache_keys = args[5], args[6]
@@ -662,20 +672,27 @@
         *pair(n_tp - 1),
         *pair(members - 1),
     ]
-    return pl.pallas_call(
+    results = pl.pallas_call(
         functools.partial(kernel, dims),
         out_shape=(
-            jax.ShapeDtypeStruct(state.shape, fl),
-            jax.ShapeDtypeStruct((ch, cache_keys.shape[1]), bf),
-            jax.ShapeDtypeStruct((ch, cache_keys.shape[1]), bf),
+            pltpu.VMEM(state.shape, fl),
+            pltpu.VMEM((ch, cache_keys.shape[1]), bf),
+            pltpu.VMEM((ch, cache_keys.shape[1]), bf),
         ),
         in_specs=[hbm] * 15,
         out_specs=(vm, vm, vm),
         scratch_shapes=scratch,
         compiler_params=pltpu.CompilerParams(
-            collective_id=0, has_side_effects=True, vmem_limit_bytes=67043328
+            collective_id=0, has_side_effects=True, vmem_limit_bytes=VMEM_LIMIT
         ),
     )(*args)
+    return pl.pallas_call(
+        write_out,
+        out_shape=tuple(jax.ShapeDtypeStruct(r.shape, r.dtype) for r in results),
+        in_specs=[vm] * 3,
+        out_specs=(hbm,) * 3,
+        scratch_shapes=[dma((3,))],
+    )(*[pltpu.with_memory_space_constraint(r, pltpu.VMEM) for r in results])
 
 
 def step(dims, *args):

time: 58.3 us -> 54.1 us (0.928)
  local copies, waits for them, and re-layouts: 4.13 us -> 0 us
    unnamed x3 -> x0, local copies, waits for them, and re-layouts: 4.13 us -> none
    pallas_call x1 -> x2, Pallas kernels: 53.3 us -> 53.3 us  [the longest x1 52.6 us: fused(): pl.pallas_call(functools.partial(kernel, dims), out_shape=(pltpu.VMEM(sta...]
where the time goes in v1:
time: 54.1 us; the launch traced here: 54 us
  Pallas kernels  53.3 us (99%)
  between operations  0.64 us (1%)
    pallas_call x1, Pallas kernels, fused(): pl.pallas_call(functools.partial(kernel, dims), out_shape=(pltpu.VMEM(sta...  52.6 us

profile of v1, /device:TPU:0, one launch (start us, length us, event | category | flops | bytes accessed | tf_op | source)
XLA Modules:
  0.0 54.0 jit_solution(6413840404689825933)
XLA Ops:
  0.6 52.6 %shard_map.166 = (f32[4,16,320]{2,1,0:T(8,128)S(1)}, bf16[16,256]{1,0:T(8,128)(2,1)S(1)}, bf16[16,256]{1,0:T(8,128)(2,1)S(1)}) custom-call(f32[4,16,320]{2,1,0:T(8,128)} %state_hbm.1, bf16[16,320]{1,0:T(8,128)(2,1)} %clean_hbm.1, bf16[2560,256]{1,0:T(8,128)(2,1)} %wq_hbm.1, bf16[2560,256]{1,0:T(8,128)(2,1)} %wk_hbm.1, bf16[2560,256]{1,0:T(8,128)(2,1)} %wv_hbm.1, ...), custom_call_target="tpu_custom_call" | custom-call | tf_op jit(solution)/shard_map/pallas_call | solution.py:675
  53.3 0.7 %shard_map.167 = (f32[4,16,320]{2,1,0:T(8,128)}, bf16[16,256]{1,0:T(8,128)(2,1)}, bf16[16,256]{1,0:T(8,128)(2,1)}) custom-call(f32[4,16,320]{2,1,0:T(8,128)S(1)} %get-tuple-element.6.refs_0_, bf16[16,256]{1,0:T(8,128)(2,1)S(1)} %get-tuple-element.7.refs_1_, bf16[16,256]{1,0:T(8,128)(2,1)S(1)} %get-tuple-element.8.refs_2_), custom_call_target="tpu_custom_call" | custom-call | tf_op jit(solution)/shard_map/pallas_call | solution.py:689

commit v2 on v1

--- a/solution.py
+++ b/solution.py
@@ -212,25 +212,37 @@
     mask_ref,
     w_buf,
     wo_buf,
+    wo_cut,
     cache_buf,
     seen_buf,
+    ssq_own,
     ssq_buf,
     ssy_buf,
-    h_own,
+    raw,
+    raw_in,
     h_buf,
     acc,
-    part,
-    part_in,
+    q_part,
+    q_in,
+    kv_part,
+    kv_send,
+    kv_in,
     kv_buf,
     fin_in,
     att_buf,
     y_part,
     y_send,
-    y_in1,
-    v_send,
-    v_in,
-    z_send,
-    z_in,
+    y_in,
+    near_a,
+    far_a,
+    cross_a,
+    za_send,
+    za_in,
+    zb_send,
+    zb_in,
+    near_b,
+    far_b,
+    cross_b,
     local_sem,
     cache_s,
     cache_r,
@@ -252,10 +264,16 @@
     t_r,
     y1_s,
     y1_r,
-    yv_s,
-    yv_r,
-    y2_s,
-    y2_r,
+    fa_s,
+    na_s,
+    xa_r,
+    za_s,
+    za_r,
+    zb_s,
+    zb_r,
+    fb_s,
+    nb_s,
+    xb_r,
     ssy_s,
     ssy_r,
 ):
@@ -264,10 +282,12 @@
     members = n_grp * n_tp
     flight, ch, width = state_hbm.shape
     rows_count = flight * ch
+    half = rows_count // 2
     all_rows = rows_count + ch
     cache_dev = ck_hbm.shape[0]
     lanes = ssq_buf.shape[2]
     total_rows = n_ctx * all_rows
+    queries = n_ctx * rows_count
     g, c, t = lax.axis_index("grp"), lax.axis_index("ctx"), lax.axis_index("tp")
     u, k = g // per, g % per
     j = g * n_tp + t
@@ -277,19 +297,34 @@
     beside = ((1 - u) * per + k, c, t)
     held = 1 - u
     at_home = u == c
-    cross = ((1 - u) * per + k, other, t)
+    owner = (c * per + k, other, t)
 
     def member(index):
         return (index // n_tp, c, index % n_tp)
 
-    def zpeer(d):
-        return (g, c, (t + d) % n_tp)
+    side = t // (n_tp // 2)
+    inner = t + side * (n_tp - 1 - 2 * t)
+    peers = []
+    for i in range(n_tp - 1):
+        v = n_tp - 1 - i
+        p = v - (inner - v + n_tp) // n_tp
+        peers.append(p + side * (n_tp - 1 - 2 * p))
+    places = [t] + peers
+
+    def zpeer(tt):
+        return (g, c, tt)
 
     barrier = pltpu.get_barrier_semaphore()
-    for d in range(1, members):
-        pl.semaphore_signal(barrier, inc=1, device_id=member((j + d) % members), device_id_type=MESH)
-    pl.semaphore_signal(barrier, inc=1, device_id=partner, device_id_type=MESH)
-    pl.semaphore_signal(barrier, inc=1, device_id=cross, device_id_type=MESH)
+    for dg in range(n_grp):
+        for dc in range(n_ctx):
+            for dt in range(n_tp):
+                if dg + dc + dt > 0:
+                    pl.semaphore_signal(
+                        barrier,
+                        inc=1,
+                        device_id=((g + dg) % n_grp, (c + dc) % n_ctx, (t + dt) % n_tp),
+                        device_id_type=MESH,
+                    )
 
     loads = [
         pltpu.make_async_copy(wq_hbm, w_buf.at[0], local_sem.at[0]),
@@ -327,28 +362,45 @@
     rows = jnp.concatenate(
         [state_ref[...].reshape(rows_count, width), clean_ref[...].astype(jnp.float32)], axis=0
     )
-    ssq_buf[0] = row_squares(rows, lanes)[0:1]
+    ssq_own[...] = row_squares(rows, lanes)[0:1]
+
+    @pl.when(c == held)
+    def _():
+        ssq_buf[j] = ssq_own[...]
+
+    modulation = mg_ref[...].reshape(1, width)
+    gained = rows * ng_ref[...].reshape(1, width)
+    for f in range(flight):
+        sigma = levels_ref[noise_ref[f]]
+        raw[f * ch : (f + 1) * ch] = gained[f * ch : (f + 1) * ch] * (1.0 + sigma * modulation)
+    raw[rows_count:] = gained[rows_count:]
     line = lax.broadcasted_iota(jnp.int32, (8, SLOT), 0)
     for s in range(cache_dev // SLOT):
         block = jnp.zeros((8, SLOT), jnp.float32)
         for f in range(flight):
-            shown = jnp.where(mask_ref[f, place_ref[s]] != 0, 1.0, 0.0)
-            block = jnp.where(line == f, shown, block)
+            hidden = jnp.where(mask_ref[f, place_ref[s]] != 0, 0.0, -jnp.inf)
+            block = jnp.where(line == f, hidden, block)
         seen_buf[c, :, s * SLOT : (s + 1) * SLOT] = block
-    pl.semaphore_wait(barrier, members + 1)
-
-    def exchange(buf, send, recv):
-        copies = [
-            remote(
-                buf.at[0], buf.at[d], send.at[d - 1], recv.at[d - 1], member((j + d) % members)
-            )
-            for d in range(1, members)
-        ]
-        for copy in copies:
-            copy.start()
-        return copies
-
-    ssq_copies = exchange(ssq_buf, ssq_s, ssq_r)
+    pl.semaphore_wait(barrier, n_grp * n_ctx * n_tp - 1)
+
+    ssq_copies = []
+    for dk in range(per):
+        for dc in range(n_ctx):
+            for dt in range(n_tp):
+                copy = remote(
+                    ssq_own,
+                    ssq_buf.at[j],
+                    ssq_s.at[len(ssq_copies)],
+                    ssq_r.at[j],
+                    ((1 - c) * per + (k + dk) % per, (c + dc) % n_ctx, (t + dt) % n_tp),
+                )
+                if ssq_copies:
+                    copy.start()
+                else:
+                    pl.when(c != held)(copy.start)
+                ssq_copies.append(copy)
+    a_copy = remote(raw, raw_in, a_s.at[0], a_r.at[0], ((1 - c) * per + k, u, t))
+    a_copy.start()
     cache_copies = [
         remote(seen_buf.at[c], seen_buf.at[c], cache_s.at[0], cache_r.at[0], partner),
         remote(
@@ -358,56 +410,52 @@
             cv_hbm.at[:, other_lanes], cache_buf.at[1, c], cache_s.at[2], cache_r.at[2], partner
         ),
     ]
-    for copy in cache_copies[:2]:
+    for copy in cache_copies:
         copy.start()
-    for copy in ssq_copies:
-        copy.wait_recv()
+
+    def ssq_arrival(a, b):
+        source = (g + a) % n_grp * n_tp + (t + b) % n_tp
+        return remote(ssq_own, ssq_buf.at[source], ssq_s.at[0], ssq_r.at[source], partner)
+
+    for a in range(n_grp):
+        for b in range(n_tp):
+            if a + b > 0:
+                ssq_arrival(a, b).wait_recv()
+            else:
+                pl.when(c != held)(ssq_arrival(a, b).wait_recv)
 
     total = ssq_buf[0]
     for d in range(1, members):
         total = total + ssq_buf[d]
     inverse = lax.rsqrt(jnp.transpose(jnp.broadcast_to(total, (8, lanes)))[:all_rows, 0:1] / D + epsilon)
-    modulation = mg_ref[...].reshape(1, width)
-    scaled = rows * inverse * ng_ref[...].reshape(1, width)
-    blocks = []
-    for f in range(flight):
-        sigma = levels_ref[noise_ref[f]]
-        blocks.append(scaled[f * ch : (f + 1) * ch] * (1.0 + sigma * modulation))
-    blocks.append(scaled[rows_count:])
-    features = jnp.concatenate(blocks, axis=0).astype(jnp.bfloat16)
-    h_own[...] = features
-
+    a_copy.wait_recv()
     mine = k * n_tp + t
-    a_copy = remote(
-        h_own, h_buf.at[mine, c], a_s.at[0], a_r.at[0], ((1 - c) * per + k, u, t)
-    )
-    a_copy.start()
-    cache_copies[2].start()
-    remote(h_own, h_buf.at[mine, held], a_s.at[0], a_r.at[0], partner).wait_recv()
+    h_buf[mine, held] = (raw_in[...] * inverse).astype(jnp.bfloat16)
 
     stage_b = []
 
-    def forward(x, index, send, recv, where, device):
-        copy = remote(h_buf.at[index, x], h_buf.at[index, x], send.at[where], recv.at[where], device)
+    def forward(x, index, send, recv, out, into, device):
+        copy = remote(h_buf.at[index, x], h_buf.at[index, x], send.at[out], recv.at[into], device)
         copy.start()
         stage_b.append(copy)
 
-    def arrived(x, index, send, recv, where, device):
+    def arrived(x, index, send, recv, into, device):
         remote(
-            h_buf.at[index, x], h_buf.at[index, x], send.at[where], recv.at[where], device
+            h_buf.at[index, x], h_buf.at[index, x], send.at[0], recv.at[into], device
         ).wait_recv()
 
-    def slot_of(core, d):
-        return core * n_tp + (t + n_tp - d) % n_tp
-
-    for d in range(1, n_tp):
-        forward(held, mine, b_s, b_r, d - 1, zpeer(d))
-    forward(held, mine, n_s, n_r, 0, beside)
-    forward(held, mine, c_s, c_r, 0, sibling)
-    for d in range(1, n_tp):
-        arrived(held, slot_of(k, d), b_s, b_r, d - 1, zpeer(d))
-        forward(held, slot_of(k, d), n_s, n_r, d, beside)
-        forward(held, slot_of(k, d), c_s, c_r, d, sibling)
+    for i, tt in enumerate(peers):
+        forward(held, mine, b_s, b_r, i, t, zpeer(tt))
+    forward(held, mine, n_s, n_r, 0, t, beside)
+    forward(held, mine, c_s, c_r, 0, t, sibling)
+
+    loads[3].wait()
+    for block in range(per * n_tp):
+        wo_cut[block] = wo_buf[:, block * width : (block + 1) * width]
+    for i, tt in enumerate(peers):
+        arrived(held, k * n_tp + tt, b_s, b_r, tt, zpeer(tt))
+        forward(held, k * n_tp + tt, n_s, n_r, i + 1, tt, beside)
+        forward(held, k * n_tp + tt, c_s, c_r, i + 1, tt, sibling)
 
     for copy in loads[:3]:
         copy.wait()
@@ -417,43 +465,60 @@
         depth = pl.ds(pl.multiple_of(slot * width, 64), width)
         return jnp.dot(lhs, w_buf[i, depth, :], preferred_element_type=jnp.float32)
 
-    for d in range(n_tp):
-        slot = slot_of(k, d)
-        arrived(u, slot, n_s, n_r, d, beside)
-        forward(u, slot, c_s, c_r, n_tp + d, sibling)
-        for i in range(3):
-            acc[i] = project(slot, i) if d == 0 else acc[i] + project(slot, i)
+    def own_slot(i):
+        tt = places[i]
+        slot = k * n_tp + tt
+        arrived(u, slot, n_s, n_r, tt, beside)
+        forward(u, slot, c_s, c_r, n_tp + i, n_tp + tt, sibling)
+        for w in range(3):
+            acc[w] = project(slot, w) if i == 0 else acc[w] + project(slot, w)
+
     part_copies = []
-    for d in range(n_tp):
-        slot = slot_of(1 - k, d)
-        arrived(held, slot, c_s, c_r, d, sibling)
-        arrived(u, slot, c_s, c_r, n_tp + d, sibling)
-        for i in range(3):
-            if d < n_tp - 1:
-                acc[i] = acc[i] + project(slot, i)
+
+    def sibling_slot(i):
+        tt = places[i]
+        slot = (1 - k) * n_tp + tt
+        arrived(held, slot, c_s, c_r, tt, sibling)
+        arrived(u, slot, c_s, c_r, n_tp + tt, sibling)
+        for w in range(3):
+            if i < n_tp - 1:
+                acc[w] = acc[w] + project(slot, w)
                 continue
-            whole = acc[i] + project(slot, i)
+            whole = acc[w] + project(slot, w)
             for head in range(n_ctx):
-                part[head, i] = whole[:, head * HD : (head + 1) * HD]
-            copy = remote(part.at[other, i], part_in.at[i], p_s.at[i], p_r.at[i], partner)
+                piece = whole[:, head * HD : (head + 1) * HD]
+                if w == 0:
+                    for x in range(n_ctx):
+                        q_part[head, x * rows_count : (x + 1) * rows_count] = piece[
+                            x * all_rows : x * all_rows + rows_count
+                        ]
+                else:
+                    kv_part[head, w - 1] = piece
+                    kv_send[head, w - 1] = piece.astype(jnp.bfloat16)
+            if w == 0:
+                copy = remote(q_part.at[other], q_in, p_s.at[0], p_r.at[0], partner)
+            else:
+                copy = remote(
+                    kv_send.at[other, w - 1], kv_in.at[w - 1], p_s.at[w], p_r.at[w], partner
+                )
             copy.start()
             part_copies.append(copy)
+
+    for i in range(n_tp):
+        own_slot(i)
+        if i > 0:
+            sibling_slot(i - 1)
+    sibling_slot(n_tp - 1)
     for copy in cache_loads:
         copy.wait()
-    for i, copy in enumerate(cache_copies):
+    for copy in cache_copies:
         copy.wait_recv()
-    row_group = (lax.broadcasted_iota(jnp.int32, (total_rows, 8), 0) % all_rows) // ch
-    pick = (row_group == lax.broadcasted_iota(jnp.int32, (total_rows, 8), 1)).astype(jnp.bfloat16)
-    seen = [
-        jnp.dot(pick, seen_buf[x].astype(jnp.bfloat16), preferred_element_type=jnp.float32) > 0.5
-        for x in range(n_ctx)
-    ]
-    query_group = (lax.broadcasted_iota(jnp.int32, (total_rows, total_rows), 0) % all_rows) // ch
-    key_group = (lax.broadcasted_iota(jnp.int32, (total_rows, total_rows), 1) % all_rows) // ch
-    seen.append(jnp.logical_or(key_group == flight, key_group <= query_group))
+    query_group = (lax.broadcasted_iota(jnp.int32, (queries, total_rows), 0) % rows_count) // ch
+    key_group = (lax.broadcasted_iota(jnp.int32, (queries, total_rows), 1) % all_rows) // ch
+    flight_seen = jnp.logical_or(key_group == flight, key_group <= query_group)
 
     part_copies[0].wait_recv()
-    q = (part[c, 0] + part_in[0]).astype(jnp.bfloat16)
+    q = (q_part[c] + q_in[...]).astype(jnp.bfloat16)
     scale = 1.0 / math.sqrt(HD)
 
     def score(keys):
@@ -462,29 +527,34 @@
             * scale
         )
 
-    scores = [score(cache_buf[0, x]) for x in range(n_ctx)]
+    scores = []
+    for x in range(n_ctx):
+        plain = score(cache_buf[0, x])
+        scores.append(
+            jnp.concatenate(
+                [
+                    plain[b * ch : (b + 1) * ch] + seen_buf[x, b % flight : b % flight + 1]
+                    for b in range(n_ctx * flight)
+                ],
+                axis=0,
+            )
+        )
+    peak = jnp.max(jnp.maximum(scores[0], scores[1]), axis=1, keepdims=True)
     part_copies[1].wait_recv()
-    key = (part[c, 1] + part_in[1]).astype(jnp.bfloat16)
-    scores.append(score(key))
-    scores = [jnp.where(s, v, -jnp.inf) for s, v in zip(seen, scores)]
-    peak = functools.reduce(
-        jnp.maximum, [jnp.max(v, axis=1, keepdims=True) for v in scores]
-    )
-    weights = [
-        jnp.where(s, jnp.exp(v - peak), 0.0).astype(jnp.bfloat16) for s, v in zip(seen, scores)
-    ]
+    key = (kv_part[c, 0] + kv_in[0].astype(jnp.float32)).astype(jnp.bfloat16)
+    scores.append(jnp.where(flight_seen, score(key), -jnp.inf))
+    peak = jnp.maximum(peak, jnp.max(scores[-1], axis=1, keepdims=True))
+    weights = [jnp.exp(v - peak).astype(jnp.bfloat16) for v in scores]
     denom = sum(jnp.sum(w.astype(jnp.float32), axis=1, keepdims=True) for w in weights)
+    numer = sum(
+        jnp.dot(weights[x], cache_buf[1, x], preferred_element_type=jnp.float32)
+        for x in range(n_ctx)
+    )
     part_copies[2].wait_recv()
-    value = (part[c, 2] + part_in[2]).astype(jnp.bfloat16)
-    values = [cache_buf[1, x] for x in range(n_ctx)] + [value]
-    numer = sum(
-        jnp.dot(w, v, preferred_element_type=jnp.float32) for w, v in zip(weights, values)
-    )
+    value = (kv_part[c, 1] + kv_in[1].astype(jnp.float32)).astype(jnp.bfloat16)
+    numer = numer + jnp.dot(weights[-1], value, preferred_element_type=jnp.float32)
     attention = (numer / denom).astype(jnp.bfloat16)
-    for x in range(n_ctx):
-        att_buf[c, x * rows_count : (x + 1) * rows_count, :] = attention[
-            x * all_rows : x * all_rows + rows_count
-        ]
+    att_buf[c] = attention
     att_copy = remote(att_buf.at[c], att_buf.at[c], t_s.at[0], t_r.at[0], partner)
     att_copy.start()
 
@@ -497,91 +567,128 @@
     nk_ref[:, own_lanes] = kv_buf[c, 0]
     nv_ref[:, own_lanes] = kv_buf[c, 1]
 
-    loads[3].wait()
+    own_depth = pl.ds(pl.multiple_of(c * HD, HD), HD)
+    other_depth = pl.ds(pl.multiple_of(other * HD, HD), HD)
+    blocks = [(1 - k) * n_tp + tt for tt in peers + [t]] + [k * n_tp + tt for tt in peers + [t]]
+    for block in blocks:
+        y_part[block] = jnp.dot(
+            attention, wo_cut[block, own_depth, :], preferred_element_type=jnp.float32
+        )
     att_copy.wait_recv()
-    both = jnp.concatenate([att_buf[x] for x in range(n_ctx)], axis=1)
+    theirs = att_buf[other]
     y1 = []
-    for tt in range(n_tp):
-        for kk in range(per):
-            start = (kk * n_tp + tt) * width
-            piece = jnp.dot(
-                both, wo_buf[:, start : start + width], preferred_element_type=jnp.float32
-            )
-            for x in range(n_ctx):
-                half = piece[x * rows_count : (x + 1) * rows_count]
-                y_part[kk, tt, x] = half
-                y_send[kk, tt, x] = half.astype(jnp.bfloat16)
-        copy = remote(y_send.at[1 - k, tt], y_in1.at[tt], y1_s.at[tt], y1_r.at[tt], sibling)
+    for i, block in enumerate(blocks):
+        piece = y_part[block] + jnp.dot(
+            theirs, wo_cut[block, other_depth, :], preferred_element_type=jnp.float32
+        )
+        if i >= n_tp:
+            y_part[block] = piece
+            continue
+        tt = (peers + [t])[i]
+        y_send[i] = piece.astype(jnp.bfloat16)
+        copy = remote(y_send.at[i], y_in.at[tt], y1_s.at[i], y1_r.at[tt], sibling)
         copy.start()
         y1.append(copy)
-    yv = []
-    near = []
-    for d in range(1, n_tp + 1):
-        tt = (t + d) % n_tp
-        remote(
-            y_send.at[1 - k, tt], y_in1.at[tt], y1_s.at[tt], y1_r.at[tt], sibling
-        ).wait_recv()
-        for i, x in enumerate((other, c)):
-            v_send[i, d - 1] = (y_part[k, tt, x] + y_in1[tt, x].astype(jnp.float32)).astype(
-                jnp.bfloat16
-            )
-            copy = remote(
-                v_send.at[i, d - 1],
-                v_in.at[u, d - 1],
-                yv_s.at[i * n_tp + d - 1],
-                yv_r.at[u * n_tp + d - 1],
-                (c * per + k, other, t) if i == 0 else beside,
-            )
-            if i == 0:
-                copy.start()
-                yv.append(copy)
-            else:
-                near.append(copy)
-                pl.when(jnp.logical_not(at_home))(copy.start)
+    far, near, zb = [], [], []
+    for i, tt in enumerate(peers + [t]):
+        remote(y_send.at[i], y_in.at[tt], y1_s.at[i], y1_r.at[tt], sibling).wait_recv()
+        block = k * n_tp + tt
+
+        def chunk(x, start):
+            at = pl.ds(pl.multiple_of(x * rows_count + start, half), half)
+            return y_part[block, at, :] + y_in[tt, at, :].astype(jnp.float32)
+
+        far_a[i] = chunk(other, 0).astype(jnp.bfloat16)
+        copy = remote(far_a.at[i], cross_a.at[u, tt], fa_s.at[i], xa_r.at[u, tt], owner)
+        copy.start()
+        far.append(copy)
+        near_a[i] = chunk(c, 0).astype(jnp.bfloat16)
+        copy = remote(near_a.at[i], cross_a.at[u, tt], na_s.at[i], xa_r.at[u, tt], beside)
+        near.append(copy)
+        pl.when(jnp.logical_not(at_home))(copy.start)
+
+        if i < n_tp - 1:
+            for x in range(n_ctx):
+                zb_send[i, x] = chunk(x, half).astype(jnp.bfloat16)
+            copy = remote(zb_send.at[i], zb_in.at[t], zb_s.at[i], zb_r.at[t], zpeer(tt))
+            copy.start()
+            zb.append(copy)
+
     fin_copy.wait_recv()
     nk_ref[:, other_lanes] = fin_in[0]
     nv_ref[:, other_lanes] = fin_in[1]
-    y2 = []
-    for d in range(1, n_tp + 1):
+    za = []
+    for i, tt in enumerate(peers + [t]):
 
         @pl.when(at_home)
         def _():
-            v_in[u, d - 1] = v_send[1, d - 1]
+            cross_a[u, tt] = near_a[i]
 
         for y in range(n_ctx):
 
             @pl.when(jnp.logical_not(jnp.logical_and(at_home, u == y)))
             def _():
-                remote(
-                    v_send.at[0, d - 1],
-                    v_in.at[y, d - 1],
-                    yv_s.at[d - 1],
-                    yv_r.at[y * n_tp + d - 1],
-                    partner,
-                ).wait_recv()
-
-        summed = v_in[0, d - 1].astype(jnp.float32) + v_in[1, d - 1].astype(jnp.float32)
-        if d < n_tp:
-            z_send[d - 1] = summed.astype(jnp.bfloat16)
-            copy = remote(
-                z_send.at[d - 1], z_in.at[d - 1], y2_s.at[d - 1], y2_r.at[d - 1], zpeer(d)
-            )
+                remote(far_a.at[i], cross_a.at[y, tt], fa_s.at[i], xa_r.at[y, tt], partner).wait_recv()
+
+        summed_a = cross_a[0, tt].astype(jnp.float32) + cross_a[1, tt].astype(jnp.float32)
+        if i < n_tp - 1:
+            za_send[i] = summed_a.astype(jnp.bfloat16)
+            copy = remote(za_send.at[i], za_in.at[t], za_s.at[i], za_r.at[t], zpeer(tt))
             copy.start()
-            y2.append(copy)
-    for d in range(1, n_tp):
-        y2[d - 1].wait_recv()
-        summed = summed + z_in[d - 1].astype(jnp.float32)
-    y_rows = summed
+            za.append(copy)
+
+    for i, tt in enumerate(peers):
+        remote(zb_send.at[i], zb_in.at[tt], zb_s.at[i], zb_r.at[tt], zpeer(tt)).wait_recv()
+
+    def gathered(x):
+        at = pl.ds(pl.multiple_of(x * rows_count + half, half), half)
+        block = k * n_tp + t
+        result = y_part[block, at, :] + y_in[t, at, :].astype(jnp.float32)
+        for tt in peers:
+            result = result + zb_in[tt, x].astype(jnp.float32)
+        return result.astype(jnp.bfloat16)
+
+    far_b[...] = gathered(other)
+    far_copy = remote(far_b, cross_b.at[u], fb_s.at[0], xb_r.at[u], owner)
+    far_copy.start()
+    near_b[...] = gathered(c)
+    near_copy = remote(near_b, cross_b.at[u], nb_s.at[0], xb_r.at[u], beside)
+    pl.when(jnp.logical_not(at_home))(near_copy.start)
+
+    for i, tt in enumerate(peers):
+        remote(za_send.at[i], za_in.at[tt], za_s.at[i], za_r.at[tt], zpeer(tt)).wait_recv()
+        summed_a = summed_a + za_in[tt].astype(jnp.float32)
+
+    @pl.when(at_home)
+    def _():
+        cross_b[u] = near_b[...]
+
+    for y in range(n_ctx):
+
+        @pl.when(jnp.logical_not(jnp.logical_and(at_home, u == y)))
+        def _():
+            remote(far_b, cross_b.at[y], fb_s.at[0], xb_r.at[y], partner).wait_recv()
+
+    summed_b = cross_b[0].astype(jnp.float32) + cross_b[1].astype(jnp.float32)
+    y_rows = jnp.concatenate([summed_a, summed_b], axis=0)
     ssy_buf[0] = row_squares(y_rows, lanes)[0:1]
-    ssy_copies = exchange(ssy_buf, ssy_s, ssy_r)
-    for copy in ssq_copies + cache_copies + stage_b + part_copies + y1 + yv + y2:
+    ssy_copies = [
+        remote(
+            ssy_buf.at[0], ssy_buf.at[d], ssy_s.at[d - 1], ssy_r.at[d - 1], member((j + d) % members)
+        )
+        for d in range(1, members)
+    ]
+    for copy in ssy_copies:
+        copy.start()
+    pl.when(c != held)(ssq_copies[0].wait_send)
+    for copy in ssq_copies[1:] + cache_copies + stage_b + part_copies + y1 + far + zb + za:
         copy.wait_send()
-    for copy in [a_copy, att_copy, fin_copy]:
+    for copy in [a_copy, att_copy, fin_copy, far_copy]:
         copy.wait_send()
 
     @pl.when(jnp.logical_not(at_home))
     def _():
-        for copy in near:
+        for copy in near + [near_copy]:
             copy.wait_send()
 
     for copy in ssy_copies:
@@ -616,6 +723,7 @@
     members = n_grp * n_tp
     flight, ch, width = state.shape
     rows_count = flight * ch
+    half = rows_count // 2
     all_rows = rows_count + ch
     total = n_ctx * all_rows
     lanes = -(-all_rows // 128) * 128
@@ -638,38 +746,56 @@
         *[pltpu.SMEM(a.shape, a.dtype) for a in args[11:]],
         pltpu.VMEM((3,) + w_query.shape, bf),
         pltpu.VMEM(w_out.shape, bf),
+        pltpu.VMEM((per * n_tp, w_out.shape[0], width), bf),
         pltpu.VMEM((2, n_ctx, cache_dev, HD), bf),
         pltpu.VMEM((n_ctx, 8, cache_dev), fl),
+        pltpu.VMEM((1, lanes), fl),
         pltpu.VMEM((members, 1, lanes), fl),
         pltpu.VMEM((members, 1, lanes), fl),
-        pltpu.VMEM((all_rows, width), bf),
+        pltpu.VMEM((all_rows, width), fl),
+        pltpu.VMEM((all_rows, width), fl),
         pltpu.VMEM((per * n_tp, n_ctx, all_rows, width), bf),
         pltpu.VMEM((3, total, n_ctx * HD), fl),
-        pltpu.VMEM((n_ctx, 3, total, HD), fl),
-        pltpu.VMEM((3, total, HD), fl),
+        pltpu.VMEM((n_ctx, queries, HD), fl),
+        pltpu.VMEM((queries, HD), fl),
+        pltpu.VMEM((n_ctx, 2, total, HD), fl),
+        pltpu.VMEM((n_ctx, 2, total, HD), bf),
+        pltpu.VMEM((2, total, HD), bf),
         pltpu.VMEM((n_ctx, 2, ch, HD), bf),
         pltpu.VMEM((2, ch, HD), bf),
         pltpu.VMEM((n_ctx, queries, HD), bf),
-        pltpu.VMEM((per, n_tp, n_ctx, rows_count, width), fl),
-        pltpu.VMEM((per, n_tp, n_ctx, rows_count, width), bf),
-        pltpu.VMEM((n_tp, n_ctx, rows_count, width), bf),
-        pltpu.VMEM((n_ctx, n_tp, rows_count, width), bf),
-        pltpu.VMEM((n_ctx, n_tp, rows_count, width), bf),
-        pltpu.VMEM((n_tp - 1, rows_count, width), bf),
-        pltpu.VMEM((n_tp - 1, rows_count, width), bf),
+        pltpu.VMEM((per * n_tp, queries, width), fl),
+        pltpu.VMEM((n_tp, queries, width), bf),
+        pltpu.VMEM((n_tp, queries, width), bf),
+        pltpu.VMEM((n_tp, half, width), bf),
+        pltpu.VMEM((n_tp, half, width), bf),
+        pltpu.VMEM((n_ctx, n_tp, half, width), bf),
+        pltpu.VMEM((n_tp - 1, half, width), bf),
+        pltpu.VMEM((n_tp, half, width), bf),
+        pltpu.VMEM((n_tp - 1, n_ctx, half, width), bf),
+        pltpu.VMEM((n_tp, n_ctx, half, width), bf),
+        pltpu.VMEM((half, width), bf),
+        pltpu.VMEM((half, width), bf),
+        pltpu.VMEM((n_ctx, half, width), bf),
         dma((15,)),
         *pair(3),
-        *pair(members - 1),
+        *pair(members),
         *pair(1),
-        *pair(n_tp - 1),
+        *pair(n_tp),
         *pair(n_tp),
         *pair(2 * n_tp),
         *pair(3),
         *pair(1),
         *pair(1),
         *pair(n_tp),
-        *pair(n_ctx * n_tp),
-        *pair(n_tp - 1),
+        dma((n_tp,)),
+        dma((n_tp,)),
+        dma((n_ctx, n_tp)),
+        *pair(n_tp),
+        *pair(n_tp),
+        dma((1,)),
+        dma((1,)),
+        dma((n_ctx,)),
         *pair(members - 1),
     ]
     results = pl.pallas_call(

time: 54.1 us -> 51 us (0.943)
  Pallas kernels: 53.3 us -> 50.2 us
    pallas_call x1, Pallas kernels: 52.6 us -> 49.5 us  [fused(): pl.pallas_call(functools.partial(kernel, dims), out_shape=(pltpu.VMEM(sta...]
where the time goes in v2:
time: 51 us; the launch traced here: 50.8 us
  Pallas kernels  50.2 us (98%)
  between operations  0.64 us (1%)
    pallas_call x1, Pallas kernels, fused(): pl.pallas_call(functools.partial(kernel, dims), out_shape=(pltpu.VMEM(sta...  49.5 us

profile of v2, /device:TPU:0, one launch (start us, length us, event | category | flops | bytes accessed | tf_op | source)
XLA Modules:
  0.0 50.8 jit_solution(12368319684893149274)
XLA Ops:
  0.6 49.5 %shard_map.166 = (f32[4,16,320]{2,1,0:T(8,128)S(1)}, bf16[16,256]{1,0:T(8,128)(2,1)S(1)}, bf16[16,256]{1,0:T(8,128)(2,1)S(1)}) custom-call(f32[4,16,320]{2,1,0:T(8,128)} %state_hbm.1, bf16[16,320]{1,0:T(8,128)(2,1)} %clean_hbm.1, bf16[2560,256]{1,0:T(8,128)(2,1)} %wq_hbm.1, bf16[2560,256]{1,0:T(8,128)(2,1)} %wk_hbm.1, bf16[2560,256]{1,0:T(8,128)(2,1)} %wv_hbm.1, ...), custom_call_target="tpu_custom_call" | custom-call | tf_op jit(solution)/shard_map/pallas_call | solution.py:801
  50.1 0.7 %shard_map.167 = (f32[4,16,320]{2,1,0:T(8,128)}, bf16[16,256]{1,0:T(8,128)(2,1)}, bf16[16,256]{1,0:T(8,128)(2,1)}) custom-call(f32[4,16,320]{2,1,0:T(8,128)S(1)} %get-tuple-element.6.refs_0_, bf16[16,256]{1,0:T(8,128)(2,1)S(1)} %get-tuple-element.7.refs_1_, bf16[16,256]{1,0:T(8,128)(2,1)S(1)} %get-tuple-element.8.refs_2_), custom_call_target="tpu_custom_call" | custom-call | tf_op jit(solution)/shard_map/pallas_call | solution.py:815

commit v3 on v2

--- a/solution.py
+++ b/solution.py
@@ -282,7 +282,8 @@
     members = n_grp * n_tp
     flight, ch, width = state_hbm.shape
     rows_count = flight * ch
-    half = rows_count // 2
+    first = y_rows_first(rows_count)
+    late = rows_count - first
     all_rows = rows_count + ch
     cache_dev = ck_hbm.shape[0]
     lanes = ssq_buf.shape[2]
@@ -327,19 +328,18 @@
                     )
 
     loads = [
-        pltpu.make_async_copy(wq_hbm, w_buf.at[0], local_sem.at[0]),
-        pltpu.make_async_copy(wk_hbm, w_buf.at[1], local_sem.at[1]),
-        pltpu.make_async_copy(wv_hbm, w_buf.at[2], local_sem.at[2]),
-        pltpu.make_async_copy(wo_hbm, wo_buf, local_sem.at[3]),
+        pltpu.make_async_copy(src, w_buf.at[i], local_sem.at[0])
+        for i, src in enumerate((wq_hbm, wk_hbm, wv_hbm))
     ]
+    wo_load = pltpu.make_async_copy(wo_hbm, wo_buf, local_sem.at[1])
     own_lanes = pl.ds(pl.multiple_of(c * HD, HD), HD)
     other_lanes = pl.ds(pl.multiple_of(other * HD, HD), HD)
     cache_loads = [
-        pltpu.make_async_copy(ck_hbm.at[:, own_lanes], cache_buf.at[0, c], local_sem.at[4]),
-        pltpu.make_async_copy(cv_hbm.at[:, own_lanes], cache_buf.at[1, c], local_sem.at[5]),
+        pltpu.make_async_copy(src.at[:, own_lanes], cache_buf.at[c, i], local_sem.at[2])
+        for i, src in enumerate((ck_hbm, cv_hbm))
     ]
     small = [
-        pltpu.make_async_copy(src, dst, local_sem.at[6 + i])
+        pltpu.make_async_copy(src, dst, local_sem.at[3 + i])
         for i, (src, dst) in enumerate(
             [
                 (state_hbm, state_ref),
@@ -354,7 +354,7 @@
             ]
         )
     ]
-    for copy in small + loads + cache_loads:
+    for copy in small + [wo_load] + loads + cache_loads:
         copy.start()
     for copy in small:
         copy.wait()
@@ -383,47 +383,36 @@
         seen_buf[c, :, s * SLOT : (s + 1) * SLOT] = block
     pl.semaphore_wait(barrier, n_grp * n_ctx * n_tp - 1)
 
-    ssq_copies = []
+    def ssq_copy(target):
+        return remote(ssq_own, ssq_buf.at[j], ssq_s.at[0], ssq_r.at[0], target)
+
     for dk in range(per):
         for dc in range(n_ctx):
             for dt in range(n_tp):
-                copy = remote(
-                    ssq_own,
-                    ssq_buf.at[j],
-                    ssq_s.at[len(ssq_copies)],
-                    ssq_r.at[j],
-                    ((1 - c) * per + (k + dk) % per, (c + dc) % n_ctx, (t + dt) % n_tp),
+                copy = ssq_copy(
+                    ((1 - c) * per + (k + dk) % per, (c + dc) % n_ctx, (t + dt) % n_tp)
                 )
-                if ssq_copies:
+                if dk + dc + dt > 0:
                     copy.start()
                 else:
                     pl.when(c != held)(copy.start)
-                ssq_copies.append(copy)
     a_copy = remote(raw, raw_in, a_s.at[0], a_r.at[0], ((1 - c) * per + k, u, t))
     a_copy.start()
-    cache_copies = [
-        remote(seen_buf.at[c], seen_buf.at[c], cache_s.at[0], cache_r.at[0], partner),
-        remote(
-            ck_hbm.at[:, other_lanes], cache_buf.at[0, c], cache_s.at[1], cache_r.at[1], partner
-        ),
-        remote(
-            cv_hbm.at[:, other_lanes], cache_buf.at[1, c], cache_s.at[2], cache_r.at[2], partner
-        ),
-    ]
-    for copy in cache_copies:
-        copy.start()
-
-    def ssq_arrival(a, b):
-        source = (g + a) % n_grp * n_tp + (t + b) % n_tp
-        return remote(ssq_own, ssq_buf.at[source], ssq_s.at[0], ssq_r.at[source], partner)
-
-    for a in range(n_grp):
-        for b in range(n_tp):
-            if a + b > 0:
-                ssq_arrival(a, b).wait_recv()
-            else:
-                pl.when(c != held)(ssq_arrival(a, b).wait_recv)
-
+    wo_load.wait()
+    for block in range(per * n_tp):
+        wo_cut[block] = wo_buf[:, block * width : (block + 1) * width]
+
+    def ssq_wait(finish):
+        @pl.when(c == held)
+        def _():
+            most = ssq_buf.at[: members - 1]
+            finish(remote(most, most, ssq_s.at[0], ssq_r.at[0], partner))
+
+        @pl.when(c != held)
+        def _():
+            finish(remote(ssq_buf, ssq_buf, ssq_s.at[0], ssq_r.at[0], partner))
+
+    ssq_wait(lambda copy: copy.wait_recv())
     total = ssq_buf[0]
     for d in range(1, members):
         total = total + ssq_buf[d]
@@ -432,87 +421,105 @@
     mine = k * n_tp + t
     h_buf[mine, held] = (raw_in[...] * inverse).astype(jnp.bfloat16)
 
-    stage_b = []
-
-    def forward(x, index, send, recv, out, into, device):
-        copy = remote(h_buf.at[index, x], h_buf.at[index, x], send.at[out], recv.at[into], device)
+    def slot_of(core, tt):
+        return core * n_tp + tt
+
+    def link(ref, send, recv, device):
+        return remote(ref, ref, send, recv, device)
+
+    def to_beside(x, tt):
+        link(h_buf.at[slot_of(k, tt), x], n_s.at[0], n_r.at[tt], beside).start()
+
+    def to_sibling(x, tt):
+        link(h_buf.at[slot_of(k, tt), x], c_s.at[0], c_r.at[tt], sibling).start()
+
+    for tt in peers:
+        link(h_buf.at[mine, held], b_s.at[0], b_r.at[t], zpeer(tt)).start()
+    to_beside(held, t)
+    to_sibling(held, t)
+
+    cache_copies = [
+        remote(seen_buf.at[c], seen_buf.at[c], cache_s.at[0], cache_r.at[0], partner)
+    ] + [
+        remote(
+            src.at[:, other_lanes], cache_buf.at[c, i], cache_s.at[1], cache_r.at[1], partner
+        )
+        for i, src in enumerate((ck_hbm, cv_hbm))
+    ]
+    for copy in cache_copies:
         copy.start()
-        stage_b.append(copy)
-
-    def arrived(x, index, send, recv, into, device):
-        remote(
-            h_buf.at[index, x], h_buf.at[index, x], send.at[0], recv.at[into], device
-        ).wait_recv()
-
-    for i, tt in enumerate(peers):
-        forward(held, mine, b_s, b_r, i, t, zpeer(tt))
-    forward(held, mine, n_s, n_r, 0, t, beside)
-    forward(held, mine, c_s, c_r, 0, t, sibling)
-
-    loads[3].wait()
-    for block in range(per * n_tp):
-        wo_cut[block] = wo_buf[:, block * width : (block + 1) * width]
-    for i, tt in enumerate(peers):
-        arrived(held, k * n_tp + tt, b_s, b_r, tt, zpeer(tt))
-        forward(held, k * n_tp + tt, n_s, n_r, i + 1, tt, beside)
-        forward(held, k * n_tp + tt, c_s, c_r, i + 1, tt, sibling)
-
-    for copy in loads[:3]:
-        copy.wait()
-
-    def project(slot, i):
-        lhs = h_buf[slot].reshape(total_rows, width)
-        depth = pl.ds(pl.multiple_of(slot * width, 64), width)
-        return jnp.dot(lhs, w_buf[i, depth, :], preferred_element_type=jnp.float32)
-
-    def own_slot(i):
+
+    pltpu.make_async_copy(w_buf, w_buf, local_sem.at[0]).wait()
+
+    def project(slots, w):
+        total = None
+        for slot in slots:
+            lhs = h_buf[slot].reshape(total_rows, width)
+            depth = pl.ds(pl.multiple_of(slot * width, 64), width)
+            product = jnp.dot(lhs, w_buf[w, depth, :], preferred_element_type=jnp.float32)
+            total = product if total is None else total + product
+        return total
+
+    def from_line(i):
         tt = places[i]
-        slot = k * n_tp + tt
-        arrived(u, slot, n_s, n_r, tt, beside)
-        forward(u, slot, c_s, c_r, n_tp + i, n_tp + tt, sibling)
+        link(h_buf.at[slot_of(k, tt), held], b_s.at[0], b_r.at[tt], zpeer(tt)).wait_recv()
+        to_beside(held, tt)
+        to_sibling(held, tt)
+
+    def from_beside(i):
+        tt = places[i]
+        link(h_buf.at[slot_of(k, tt), u], n_s.at[0], n_r.at[tt], beside).wait_recv()
+        to_sibling(u, tt)
+
+    def from_sibling(i):
+        tt = places[i]
+        link(h_buf.at[slot_of(1 - k, tt)], c_s.at[0], c_r.at[tt], sibling).wait_recv()
+
+    def add(slots, fresh=False):
         for w in range(3):
-            acc[w] = project(slot, w) if i == 0 else acc[w] + project(slot, w)
-
+            acc[w] = project(slots, w) if fresh else acc[w] + project(slots, w)
+
+    from_beside(0)
+    from_line(1)
+    from_sibling(0)
+    add([slot_of(k, t), slot_of(1 - k, t)], True)
+    from_line(2)
+    from_line(3)
+    from_beside(1)
+    from_beside(2)
+    from_sibling(1)
+    add([slot_of(k, places[1]), slot_of(1 - k, places[1])])
+    from_beside(3)
+    add([slot_of(k, places[2]), slot_of(k, places[3])])
+    from_sibling(2)
+    from_sibling(n_tp - 1)
     part_copies = []
-
-    def sibling_slot(i):
-        tt = places[i]
-        slot = (1 - k) * n_tp + tt
-        arrived(held, slot, c_s, c_r, tt, sibling)
-        arrived(u, slot, c_s, c_r, n_tp + tt, sibling)
-        for w in range(3):
-            if i < n_tp - 1:
-                acc[w] = acc[w] + project(slot, w)
-                continue
-            whole = acc[w] + project(slot, w)
-            for head in range(n_ctx):
-                piece = whole[:, head * HD : (head + 1) * HD]
-                if w == 0:
-                    for x in range(n_ctx):
-                        q_part[head, x * rows_count : (x + 1) * rows_count] = piece[
-                            x * all_rows : x * all_rows + rows_count
-                        ]
-                else:
-                    kv_part[head, w - 1] = piece
-                    kv_send[head, w - 1] = piece.astype(jnp.bfloat16)
+    for w in range(3):
+        whole = acc[w] + project([slot_of(1 - k, tt) for tt in places[n_tp - 2 :]], w)
+        for head in range(n_ctx):
+            piece = whole[:, head * HD : (head + 1) * HD]
             if w == 0:
-                copy = remote(q_part.at[other], q_in, p_s.at[0], p_r.at[0], partner)
+                for x in range(n_ctx):
+                    q_part[head, x * rows_count : (x + 1) * rows_count] = piece[
+                        x * all_rows : x * all_rows + rows_count
+                    ]
             else:
-                copy = remote(
-                    kv_send.at[other, w - 1], kv_in.at[w - 1], p_s.at[w], p_r.at[w], partner
-                )
-            copy.start()
-            part_copies.append(copy)
-
-    for i in range(n_tp):
-        own_slot(i)
-        if i > 0:
-            sibling_slot(i - 1)
-    sibling_slot(n_tp - 1)
-    for copy in cache_loads:
-        copy.wait()
-    for copy in cache_copies:
-        copy.wait_recv()
+                kv_part[head, w - 1] = piece
+                kv_send[head, w - 1] = piece.astype(jnp.bfloat16)
+        if w == 0:
+            copy = remote(q_part.at[other], q_in, p_s.at[0], p_r.at[0], partner)
+        else:
+            copy = remote(
+                kv_send.at[other, w - 1], kv_in.at[w - 1], p_s.at[1], p_r.at[w], partner
+            )
+        copy.start()
+        part_copies.append(copy)
+    pltpu.make_async_copy(cache_buf.at[0], cache_buf.at[0], local_sem.at[2]).wait()
+    cache_copies[0].wait_recv()
+    both_caches = remote(
+        cache_buf.at[0], cache_buf.at[0], cache_s.at[1], cache_r.at[1], partner
+    )
+    both_caches.wait_recv()
     query_group = (lax.broadcasted_iota(jnp.int32, (queries, total_rows), 0) % rows_count) // ch
     key_group = (lax.broadcasted_iota(jnp.int32, (queries, total_rows), 1) % all_rows) // ch
     flight_seen = jnp.logical_or(key_group == flight, key_group <= query_group)
@@ -529,7 +536,7 @@
 
     scores = []
     for x in range(n_ctx):
-        plain = score(cache_buf[0, x])
+        plain = score(cache_buf[x, 0])
         scores.append(
             jnp.concatenate(
                 [
@@ -547,7 +554,7 @@
     weights = [jnp.exp(v - peak).astype(jnp.bfloat16) for v in scores]
     denom = sum(jnp.sum(w.astype(jnp.float32), axis=1, keepdims=True) for w in weights)
     numer = sum(
-        jnp.dot(weights[x], cache_buf[1, x], preferred_element_type=jnp.float32)
+        jnp.dot(weights[x], cache_buf[x, 1], preferred_element_type=jnp.float32)
         for x in range(n_ctx)
     )
     part_copies[2].wait_recv()
@@ -567,132 +574,120 @@
     nk_ref[:, own_lanes] = kv_buf[c, 0]
     nv_ref[:, own_lanes] = kv_buf[c, 1]
 
-    own_depth = pl.ds(pl.multiple_of(c * HD, HD), HD)
-    other_depth = pl.ds(pl.multiple_of(other * HD, HD), HD)
-    blocks = [(1 - k) * n_tp + tt for tt in peers + [t]] + [k * n_tp + tt for tt in peers + [t]]
-    for block in blocks:
-        y_part[block] = jnp.dot(
-            attention, wo_cut[block, own_depth, :], preferred_element_type=jnp.float32
-        )
     att_copy.wait_recv()
-    theirs = att_buf[other]
-    y1 = []
-    for i, block in enumerate(blocks):
-        piece = y_part[block] + jnp.dot(
-            theirs, wo_cut[block, other_depth, :], preferred_element_type=jnp.float32
-        )
-        if i >= n_tp:
-            y_part[block] = piece
-            continue
-        tt = (peers + [t])[i]
-        y_send[i] = piece.astype(jnp.bfloat16)
-        copy = remote(y_send.at[i], y_in.at[tt], y1_s.at[i], y1_r.at[tt], sibling)
-        copy.start()
-        y1.append(copy)
-    far, near, zb = [], [], []
-    for i, tt in enumerate(peers + [t]):
-        remote(y_send.at[i], y_in.at[tt], y1_s.at[i], y1_r.at[tt], sibling).wait_recv()
-        block = k * n_tp + tt
-
-        def chunk(x, start):
-            at = pl.ds(pl.multiple_of(x * rows_count + start, half), half)
-            return y_part[block, at, :] + y_in[tt, at, :].astype(jnp.float32)
-
-        far_a[i] = chunk(other, 0).astype(jnp.bfloat16)
-        copy = remote(far_a.at[i], cross_a.at[u, tt], fa_s.at[i], xa_r.at[u, tt], owner)
-        copy.start()
-        far.append(copy)
-        near_a[i] = chunk(c, 0).astype(jnp.bfloat16)
-        copy = remote(near_a.at[i], cross_a.at[u, tt], na_s.at[i], xa_r.at[u, tt], beside)
-        near.append(copy)
-        pl.when(jnp.logical_not(at_home))(copy.start)
+    both = jnp.concatenate([att_buf[x] for x in range(n_ctx)], axis=1)
+    order = peers + [t]
+    for start in range(0, n_tp, 2):
+        for i in (start, start + 1):
+            piece = jnp.dot(
+                both, wo_cut[slot_of(1 - k, order[i])], preferred_element_type=jnp.float32
+            )
+            y_send[i] = piece.astype(jnp.bfloat16)
+        for i in (start, start + 1):
+            remote(
+                y_send.at[i], y_in.at[order[i]], y1_s.at[0], y1_r.at[order[i]], sibling
+            ).start()
+    for tt in order:
+        y_part[tt] = jnp.dot(both, wo_cut[slot_of(k, tt)], preferred_element_type=jnp.float32)
+    for i, tt in enumerate(order):
+        remote(y_send.at[i], y_in.at[tt], y1_s.at[0], y1_r.at[tt], sibling).wait_recv()
+
+        def chunk(x, start, size):
+            at = pl.ds(pl.multiple_of(x * rows_count + start, ch), size)
+            return y_part[tt, at, :] + y_in[tt, at, :].astype(jnp.float32)
+
+        far_a[i] = chunk(other, 0, first).astype(jnp.bfloat16)
+        remote(far_a.at[i], cross_a.at[tt, u], fa_s.at[0], xa_r.at[tt], owner).start()
+        near_a[i] = chunk(c, 0, first).astype(jnp.bfloat16)
+        near = remote(near_a.at[i], cross_a.at[tt, u], na_s.at[0], xa_r.at[tt], beside)
+        pl.when(jnp.logical_not(at_home))(near.start)
 
         if i < n_tp - 1:
             for x in range(n_ctx):
-                zb_send[i, x] = chunk(x, half).astype(jnp.bfloat16)
-            copy = remote(zb_send.at[i], zb_in.at[t], zb_s.at[i], zb_r.at[t], zpeer(tt))
-            copy.start()
-            zb.append(copy)
+                zb_send[i, x] = chunk(x, first, late).astype(jnp.bfloat16)
+            remote(zb_send.at[i], zb_in.at[t], zb_s.at[0], zb_r.at[0], zpeer(tt)).start()
 
     fin_copy.wait_recv()
     nk_ref[:, other_lanes] = fin_in[0]
     nv_ref[:, other_lanes] = fin_in[1]
-    za = []
-    for i, tt in enumerate(peers + [t]):
-
+
+    def both_sources(ref, send, recv):
         @pl.when(at_home)
         def _():
-            cross_a[u, tt] = near_a[i]
-
-        for y in range(n_ctx):
-
-            @pl.when(jnp.logical_not(jnp.logical_and(at_home, u == y)))
-            def _():
-                remote(far_a.at[i], cross_a.at[y, tt], fa_s.at[i], xa_r.at[y, tt], partner).wait_recv()
-
-        summed_a = cross_a[0, tt].astype(jnp.float32) + cross_a[1, tt].astype(jnp.float32)
+            remote(ref.at[0], ref.at[0], send, recv, partner).wait_recv()
+
+        @pl.when(jnp.logical_not(at_home))
+        def _():
+            remote(ref, ref, send, recv, partner).wait_recv()
+
+    for i, tt in enumerate(order):
+
+        @pl.when(at_home)
+        def _():
+            cross_a[tt, u] = near_a[i]
+
+        both_sources(cross_a.at[tt], fa_s.at[0], xa_r.at[tt])
+        summed_a = cross_a[tt, 0].astype(jnp.float32) + cross_a[tt, 1].astype(jnp.float32)
         if i < n_tp - 1:
             za_send[i] = summed_a.astype(jnp.bfloat16)
-            copy = remote(za_send.at[i], za_in.at[t], za_s.at[i], za_r.at[t], zpeer(tt))
-            copy.start()
-            za.append(copy)
-
-    for i, tt in enumerate(peers):
-        remote(zb_send.at[i], zb_in.at[tt], zb_s.at[i], zb_r.at[tt], zpeer(tt)).wait_recv()
+            remote(za_send.at[i], za_in.at[t], za_s.at[0], za_r.at[0], zpeer(tt)).start()
+
+    link(zb_send, zb_s.at[0], zb_r.at[0], partner).wait_recv()
 
     def gathered(x):
-        at = pl.ds(pl.multiple_of(x * rows_count + half, half), half)
-        block = k * n_tp + t
-        result = y_part[block, at, :] + y_in[t, at, :].astype(jnp.float32)
+        at = pl.ds(pl.multiple_of(x * rows_count + first, ch), late)
+        result = y_part[t, at, :] + y_in[t, at, :].astype(jnp.float32)
         for tt in peers:
             result = result + zb_in[tt, x].astype(jnp.float32)
         return result.astype(jnp.bfloat16)
 
     far_b[...] = gathered(other)
-    far_copy = remote(far_b, cross_b.at[u], fb_s.at[0], xb_r.at[u], owner)
+    far_copy = remote(far_b, cross_b.at[u], fb_s.at[0], xb_r.at[0], owner)
     far_copy.start()
     near_b[...] = gathered(c)
-    near_copy = remote(near_b, cross_b.at[u], nb_s.at[0], xb_r.at[u], beside)
+    near_copy = remote(near_b, cross_b.at[u], nb_s.at[0], xb_r.at[0], beside)
     pl.when(jnp.logical_not(at_home))(near_copy.start)
 
-    for i, tt in enumerate(peers):
-        remote(za_send.at[i], za_in.at[tt], za_s.at[i], za_r.at[tt], zpeer(tt)).wait_recv()
+    link(za_send, za_s.at[0], za_r.at[0], partner).wait_recv()
+    for tt in peers:
         summed_a = summed_a + za_in[tt].astype(jnp.float32)
 
     @pl.when(at_home)
     def _():
         cross_b[u] = near_b[...]
 
-    for y in range(n_ctx):
-
-        @pl.when(jnp.logical_not(jnp.logical_and(at_home, u == y)))
-        def _():
-            remote(far_b, cross_b.at[y], fb_s.at[0], xb_r.at[y], partner).wait_recv()
-
+    both_sources(cross_b, fb_s.at[0], xb_r.at[0])
     summed_b = cross_b[0].astype(jnp.float32) + cross_b[1].astype(jnp.float32)
     y_rows = jnp.concatenate([summed_a, summed_b], axis=0)
     ssy_buf[0] = row_squares(y_rows, lanes)[0:1]
-    ssy_copies = [
+    for d in range(1, members):
         remote(
-            ssy_buf.at[0], ssy_buf.at[d], ssy_s.at[d - 1], ssy_r.at[d - 1], member((j + d) % members)
-        )
-        for d in range(1, members)
-    ]
-    for copy in ssy_copies:
-        copy.start()
-    pl.when(c != held)(ssq_copies[0].wait_send)
-    for copy in ssq_copies[1:] + cache_copies + stage_b + part_copies + y1 + far + zb + za:
-        copy.wait_send()
-    for copy in [a_copy, att_copy, fin_copy, far_copy]:
+            ssy_buf.at[0], ssy_buf.at[d], ssy_s.at[0], ssy_r.at[0], member((j + d) % members)
+        ).start()
+    ssq_wait(lambda copy: copy.wait_send())
+    slots = n_tp - 1
+    for ref, send in (
+        (h_buf.at[:slots, 0], b_s),
+        (h_buf.at[: n_tp // n_ctx], n_s),
+        (h_buf.at[:n_tp], c_s),
+        (kv_send.at[0], p_s.at[1:]),
+        (y_send, y1_s),
+        (far_a, fa_s),
+        (za_send, za_s),
+        (zb_send, zb_s),
+    ):
+        link(ref, send.at[0], send.at[0], partner).wait_send()
+    for copy in [a_copy, cache_copies[0], both_caches, part_copies[0], att_copy, fin_copy, far_copy]:
         copy.wait_send()
 
     @pl.when(jnp.logical_not(at_home))
     def _():
-        for copy in near + [near_copy]:
-            copy.wait_send()
-
-    for copy in ssy_copies:
-        copy.wait_recv()
+        link(near_a, na_s.at[0], na_s.at[0], partner).wait_send()
+        near_copy.wait_send()
+
+    rest = ssy_buf.at[1:]
+    ssy_all = remote(rest, rest, ssy_s.at[0], ssy_r.at[0], partner)
+    ssy_all.wait_recv()
     total = ssy_buf[0]
     for d in range(1, members):
         total = total + ssy_buf[d]
@@ -702,8 +697,11 @@
         now = levels_ref[noise_ref[f]]
         after = levels_ref[noise_ref[f] + 1]
         out_ref[f] = state_ref[f] + (after - now) * velocity[f * ch : (f + 1) * ch]
-    for copy in ssy_copies:
-        copy.wait_send()
+    ssy_all.wait_send()
+
+
+def y_rows_first(rows_count):
+    return 3 * (rows_count // 4)
 
 
 def write_out(*refs):
@@ -723,7 +721,8 @@
     members = n_grp * n_tp
     flight, ch, width = state.shape
     rows_count = flight * ch
-    half = rows_count // 2
+    first = y_rows_first(rows_count)
+    late = rows_count - first
     all_rows = rows_count + ch
     total = n_ctx * all_rows
     lanes = -(-all_rows // 128) * 128
@@ -747,7 +746,7 @@
         pltpu.VMEM((3,) + w_query.shape, bf),
         pltpu.VMEM(w_out.shape, bf),
         pltpu.VMEM((per * n_tp, w_out.shape[0], width), bf),
-        pltpu.VMEM((2, n_ctx, cache_dev, HD), bf),
+        pltpu.VMEM((n_ctx, 2, cache_dev, HD), bf),
         pltpu.VMEM((n_ctx, 8, cache_dev), fl),
         pltpu.VMEM((1, lanes), fl),
         pltpu.VMEM((members, 1, lanes), fl),
@@ -764,39 +763,44 @@
         pltpu.VMEM((n_ctx, 2, ch, HD), bf),
         pltpu.VMEM((2, ch, HD), bf),
         pltpu.VMEM((n_ctx, queries, HD), bf),
-        pltpu.VMEM((per * n_tp, queries, width), fl),
+        pltpu.VMEM((n_tp, queries, width), fl),
         pltpu.VMEM((n_tp, queries, width), bf),
         pltpu.VMEM((n_tp, queries, width), bf),
-        pltpu.VMEM((n_tp, half, width), bf),
-        pltpu.VMEM((n_tp, half, width), bf),
-        pltpu.VMEM((n_ctx, n_tp, half, width), bf),
-        pltpu.VMEM((n_tp - 1, half, width), bf),
-        pltpu.VMEM((n_tp, half, width), bf),
-        pltpu.VMEM((n_tp - 1, n_ctx, half, width), bf),
-        pltpu.VMEM((n_tp, n_ctx, half, width), bf),
-        pltpu.VMEM((half, width), bf),
-        pltpu.VMEM((half, width), bf),
-        pltpu.VMEM((n_ctx, half, width), bf),
-        dma((15,)),
-        *pair(3),
-        *pair(members),
-        *pair(1),
-        *pair(n_tp),
-        *pair(n_tp),
-        *pair(2 * n_tp),
-        *pair(3),
+        pltpu.VMEM((n_tp, first, width), bf),
+        pltpu.VMEM((n_tp, first, width), bf),
+        pltpu.VMEM((n_tp, n_ctx, first, width), bf),
+        pltpu.VMEM((n_tp - 1, first, width), bf),
+        pltpu.VMEM((n_tp, first, width), bf),
+        pltpu.VMEM((n_tp - 1, n_ctx, late, width), bf),
+        pltpu.VMEM((n_tp, n_ctx, late, width), bf),
+        pltpu.VMEM((late, width), bf),
+        pltpu.VMEM((late, width), bf),
+        pltpu.VMEM((n_ctx, late, width), bf),
+        dma((12,)),
+        *pair(2),
         *pair(1),
         *pair(1),
-        *pair(n_tp),
+        dma((1,)),
         dma((n_tp,)),
+        dma((1,)),
         dma((n_tp,)),
-        dma((n_ctx, n_tp)),
-        *pair(n_tp),
-        *pair(n_tp),
+        dma((1,)),
+        dma((n_tp,)),
+        dma((2,)),
+        dma((3,)),
+        *pair(1),
+        *pair(1),
+        dma((1,)),
+        dma((n_tp,)),
         dma((1,)),
         dma((1,)),
-        dma((n_ctx,)),
-        *pair(members - 1),
+        dma((n_tp,)),
+        *pair(1),
+        *pair(1),
+        dma((1,)),
+        dma((1,)),
+        dma((1,)),
+        *pair(1),
     ]
     results = pl.pallas_call(
         functools.partial(kernel, dims),

time: 51 us -> 48.1 us (0.943)
  Pallas kernels: 50.2 us -> 47.3 us
    pallas_call x1, Pallas kernels: 49.5 us -> 46.6 us  [fused(): pl.pallas_call(functools.partial(kernel, dims), out_shape=(pltpu.VMEM(sta...]
where the time goes in v3:
time: 48.1 us; the launch traced here: 47.9 us
  Pallas kernels  47.3 us (98%)
  between operations  0.64 us (1%)
    pallas_call x1, Pallas kernels, fused(): pl.pallas_call(functools.partial(kernel, dims), out_shape=(pltpu.VMEM(sta...  46.6 us

profile of v3, /device:TPU:0, one launch (start us, length us, event | category | flops | bytes accessed | tf_op | source)
XLA Modules:
  0.0 47.9 jit_solution(15052497022903605449)
XLA Ops:
  0.6 46.6 %shard_map.166 = (f32[4,16,320]{2,1,0:T(8,128)S(1)}, bf16[16,256]{1,0:T(8,128)(2,1)S(1)}, bf16[16,256]{1,0:T(8,128)(2,1)S(1)}) custom-call(f32[4,16,320]{2,1,0:T(8,128)} %state_hbm.1, bf16[16,320]{1,0:T(8,128)(2,1)} %clean_hbm.1, bf16[2560,256]{1,0:T(8,128)(2,1)} %wq_hbm.1, bf16[2560,256]{1,0:T(8,128)(2,1)} %wk_hbm.1, bf16[2560,256]{1,0:T(8,128)(2,1)} %wv_hbm.1, ...), custom_call_target="tpu_custom_call" | custom-call | tf_op jit(solution)/shard_map/pallas_call | solution.py:805
  47.2 0.7 %shard_map.167 = (f32[4,16,320]{2,1,0:T(8,128)}, bf16[16,256]{1,0:T(8,128)(2,1)}, bf16[16,256]{1,0:T(8,128)(2,1)}) custom-call(f32[4,16,320]{2,1,0:T(8,128)S(1)} %get-tuple-element.6.refs_0_, bf16[16,256]{1,0:T(8,128)(2,1)S(1)} %get-tuple-element.7.refs_1_, bf16[16,256]{1,0:T(8,128)(2,1)S(1)} %get-tuple-element.8.refs_2_), custom_call_target="tpu_custom_call" | custom-call | tf_op jit(solution)/shard_map/pallas_call | solution.py:819

commit v4 on v3

--- a/solution.py
+++ b/solution.py
@@ -213,6 +213,7 @@
     w_buf,
     wo_buf,
     wo_cut,
+    wo_sib,
     cache_buf,
     seen_buf,
     ssq_own,
@@ -231,8 +232,6 @@
     fin_in,
     att_buf,
     y_part,
-    y_send,
-    y_in,
     near_a,
     far_a,
     cross_a,
@@ -262,8 +261,8 @@
     f_r,
     t_s,
     t_r,
-    y1_s,
-    y1_r,
+    wo_s,
+    wo_r,
     fa_s,
     na_s,
     xa_r,
@@ -310,7 +309,11 @@
         v = n_tp - 1 - i
         p = v - (inner - v + n_tp) // n_tp
         peers.append(p + side * (n_tp - 1 - 2 * p))
-    places = [t] + peers
+    pair = t + 1 - 2 * (t % 2)
+    span = n_tp // 2
+    across = (t + span) % n_tp
+    diagonal = (pair + span) % n_tp
+    places = [t, pair, across, diagonal]
 
     def zpeer(tt):
         return (g, c, tt)
@@ -401,6 +404,10 @@
     wo_load.wait()
     for block in range(per * n_tp):
         wo_cut[block] = wo_buf[:, block * width : (block + 1) * width]
+    wo_copy = remote(
+        wo_cut.at[pl.ds((1 - k) * n_tp, n_tp)], wo_sib, wo_s.at[0], wo_r.at[0], sibling
+    )
+    wo_copy.start()
 
     def ssq_wait(finish):
         @pl.when(c == held)
@@ -433,8 +440,11 @@
     def to_sibling(x, tt):
         link(h_buf.at[slot_of(k, tt), x], c_s.at[0], c_r.at[tt], sibling).start()
 
-    for tt in peers:
-        link(h_buf.at[mine, held], b_s.at[0], b_r.at[t], zpeer(tt)).start()
+    def to_line(tt, device):
+        link(h_buf.at[slot_of(k, tt), held], b_s.at[0], b_r.at[tt], device).start()
+
+    to_line(t, zpeer(across))
+    to_line(t, zpeer(pair))
     to_beside(held, t)
     to_sibling(held, t)
 
@@ -462,13 +472,19 @@
 
     def from_line(i):
         tt = places[i]
-        link(h_buf.at[slot_of(k, tt), held], b_s.at[0], b_r.at[tt], zpeer(tt)).wait_recv()
-        to_beside(held, tt)
+        link(h_buf.at[slot_of(k, tt), held], b_s.at[0], b_r.at[tt], partner).wait_recv()
+        if i == 1:
+            to_beside(held, tt)
+        if i == 2:
+            to_line(tt, zpeer(pair))
         to_sibling(held, tt)
 
     def from_beside(i):
         tt = places[i]
         link(h_buf.at[slot_of(k, tt), u], n_s.at[0], n_r.at[tt], beside).wait_recv()
+        if i in (0, 2):
+            device = zpeer(across if i == 0 else pair)
+            link(h_buf.at[slot_of(k, tt), u], n_s.at[0], n_r.at[tt], device).start()
         to_sibling(u, tt)
 
     def from_sibling(i):
@@ -481,21 +497,21 @@
 
     from_beside(0)
     from_line(1)
+    from_line(2)
     from_sibling(0)
     add([slot_of(k, t), slot_of(1 - k, t)], True)
-    from_line(2)
+    from_beside(2)
+    from_beside(1)
     from_line(3)
-    from_beside(1)
-    from_beside(2)
     from_sibling(1)
-    add([slot_of(k, places[1]), slot_of(1 - k, places[1])])
+    add([slot_of(k, pair), slot_of(1 - k, pair)])
     from_beside(3)
-    add([slot_of(k, places[2]), slot_of(k, places[3])])
     from_sibling(2)
+    add([slot_of(k, across), slot_of(1 - k, across), slot_of(k, diagonal)])
     from_sibling(n_tp - 1)
     part_copies = []
     for w in range(3):
-        whole = acc[w] + project([slot_of(1 - k, tt) for tt in places[n_tp - 2 :]], w)
+        whole = acc[w] + project([slot_of(1 - k, diagonal)], w)
         for head in range(n_ctx):
             piece = whole[:, head * HD : (head + 1) * HD]
             if w == 0:
@@ -561,9 +577,9 @@
     value = (kv_part[c, 1] + kv_in[1].astype(jnp.float32)).astype(jnp.bfloat16)
     numer = numer + jnp.dot(weights[-1], value, preferred_element_type=jnp.float32)
     attention = (numer / denom).astype(jnp.bfloat16)
-    att_buf[c] = attention
-    att_copy = remote(att_buf.at[c], att_buf.at[c], t_s.at[0], t_r.at[0], partner)
-    att_copy.start()
+    att_buf[k * n_ctx + c] = attention
+    for device in (partner, (u * per + (1 - k), other, t), sibling):
+        link(att_buf.at[k * n_ctx + c], t_s.at[0], t_r.at[0], device).start()
 
     for x in range(n_ctx):
         last = slice(x * all_rows + rows_count, (x + 1) * all_rows)
@@ -574,27 +590,24 @@
     nk_ref[:, own_lanes] = kv_buf[c, 0]
     nv_ref[:, own_lanes] = kv_buf[c, 1]
 
-    att_copy.wait_recv()
-    both = jnp.concatenate([att_buf[x] for x in range(n_ctx)], axis=1)
+    wo_copy.wait_recv()
+    shared = att_buf.at[: per * n_ctx - 1]
+    att_all = link(shared, t_s.at[0], t_r.at[0], partner)
+    att_all.wait_recv()
     order = peers + [t]
-    for start in range(0, n_tp, 2):
-        for i in (start, start + 1):
-            piece = jnp.dot(
-                both, wo_cut[slot_of(1 - k, order[i])], preferred_element_type=jnp.float32
-            )
-            y_send[i] = piece.astype(jnp.bfloat16)
-        for i in (start, start + 1):
-            remote(
-                y_send.at[i], y_in.at[order[i]], y1_s.at[0], y1_r.at[order[i]], sibling
-            ).start()
-    for tt in order:
-        y_part[tt] = jnp.dot(both, wo_cut[slot_of(k, tt)], preferred_element_type=jnp.float32)
+
+    def heads_of(core):
+        return jnp.concatenate([att_buf[core * n_ctx + x] for x in range(n_ctx)], axis=1)
+
+    ours, theirs = heads_of(k), heads_of(1 - k)
     for i, tt in enumerate(order):
-        remote(y_send.at[i], y_in.at[tt], y1_s.at[0], y1_r.at[tt], sibling).wait_recv()
+        y_part[i] = jnp.dot(
+            ours, wo_cut[slot_of(k, tt)], preferred_element_type=jnp.float32
+        ) + jnp.dot(theirs, wo_sib[tt], preferred_element_type=jnp.float32)
 
         def chunk(x, start, size):
             at = pl.ds(pl.multiple_of(x * rows_count + start, ch), size)
-            return y_part[tt, at, :] + y_in[tt, at, :].astype(jnp.float32)
+            return y_part[i, at, :]
 
         far_a[i] = chunk(other, 0, first).astype(jnp.bfloat16)
         remote(far_a.at[i], cross_a.at[tt, u], fa_s.at[0], xa_r.at[tt], owner).start()
@@ -636,7 +649,7 @@
 
     def gathered(x):
         at = pl.ds(pl.multiple_of(x * rows_count + first, ch), late)
-        result = y_part[t, at, :] + y_in[t, at, :].astype(jnp.float32)
+        result = y_part[n_tp - 1, at, :]
         for tt in peers:
             result = result + zb_in[tt, x].astype(jnp.float32)
         return result.astype(jnp.bfloat16)
@@ -671,13 +684,13 @@
         (h_buf.at[: n_tp // n_ctx], n_s),
         (h_buf.at[:n_tp], c_s),
         (kv_send.at[0], p_s.at[1:]),
-        (y_send, y1_s),
+        (shared, t_s),
         (far_a, fa_s),
         (za_send, za_s),
         (zb_send, zb_s),
     ):
         link(ref, send.at[0], send.at[0], partner).wait_send()
-    for copy in [a_copy, cache_copies[0], both_caches, part_copies[0], att_copy, fin_copy, far_copy]:
+    for copy in [a_copy, cache_copies[0], both_caches, part_copies[0], wo_copy, fin_copy, far_copy]:
         copy.wait_send()
 
     @pl.when(jnp.logical_not(at_home))
@@ -746,6 +759,7 @@
         pltpu.VMEM((3,) + w_query.shape, bf),
         pltpu.VMEM(w_out.shape, bf),
         pltpu.VMEM((per * n_tp, w_out.shape[0], width), bf),
+        pltpu.VMEM((n_tp, w_out.shape[0], width), bf),
         pltpu.VMEM((n_ctx, 2, cache_dev, HD), bf),
         pltpu.VMEM((n_ctx, 8, cache_dev), fl),
         pltpu.VMEM((1, lanes), fl),
@@ -762,10 +776,8 @@
         pltpu.VMEM((2, total, HD), bf),
         pltpu.VMEM((n_ctx, 2, ch, HD), bf),
         pltpu.VMEM((2, ch, HD), bf),
-        pltpu.VMEM((n_ctx, queries, HD), bf),
+        pltpu.VMEM((per * n_ctx, queries, HD), bf),
         pltpu.VMEM((n_tp, queries, width), fl),
-        pltpu.VMEM((n_tp, queries, width), bf),
-        pltpu.VMEM((n_tp, queries, width), bf),
         pltpu.VMEM((n_tp, first, width), bf),
         pltpu.VMEM((n_tp, first, width), bf),
         pltpu.VMEM((n_tp, n_ctx, first, width), bf),
@@ -790,8 +802,7 @@
         dma((3,)),
         *pair(1),
         *pair(1),
-        dma((1,)),
-        dma((n_tp,)),
+        *pair(1),
         dma((1,)),
         dma((1,)),
         dma((n_tp,)),
@@ -828,7 +839,7 @@
 def step(dims, *args):
     n_grp, n_ctx, n_tp = dims
     heads_dev = args[6].shape[1] // HD
-    if n_ctx == heads_dev == 2 and n_grp == 2 * n_ctx and args[0].shape[0] <= 8:
+    if n_ctx == heads_dev == 2 and n_grp == n_tp == 4 and args[0].shape[0] == 4:
         return fused(dims, *args)
     return local(*args)
 

time: 48.1 us -> 47.1 us (0.979)
  Pallas kernels: 47.3 us -> 46.3 us
    pallas_call x1, Pallas kernels: 46.6 us -> 45.6 us  [fused(): pl.pallas_call(functools.partial(kernel, dims), out_shape=(pltpu.VMEM(sta...]
where the time goes in v4:
time: 47.1 us; the launch traced here: 46.9 us
  Pallas kernels  46.3 us (98%)
  between operations  0.64 us (1%)
    pallas_call x1, Pallas kernels, fused(): pl.pallas_call(functools.partial(kernel, dims), out_shape=(pltpu.VMEM(sta...  45.6 us

profile of v4, /device:TPU:0, one launch (start us, length us, event | category | flops | bytes accessed | tf_op | source)
XLA Modules:
  0.0 46.9 jit_solution(14576150148891316118)
XLA Ops:
  0.6 45.6 %shard_map.166 = (f32[4,16,320]{2,1,0:T(8,128)S(1)}, bf16[16,256]{1,0:T(8,128)(2,1)S(1)}, bf16[16,256]{1,0:T(8,128)(2,1)S(1)}) custom-call(f32[4,16,320]{2,1,0:T(8,128)} %state_hbm.1, bf16[16,320]{1,0:T(8,128)(2,1)} %clean_hbm.1, bf16[2560,256]{1,0:T(8,128)(2,1)} %wq_hbm.1, bf16[2560,256]{1,0:T(8,128)(2,1)} %wk_hbm.1, bf16[2560,256]{1,0:T(8,128)(2,1)} %wv_hbm.1, ...), custom_call_target="tpu_custom_call" | custom-call | tf_op jit(solution)/shard_map/pallas_call | solution.py:816
  46.3 0.7 %shard_map.167 = (f32[4,16,320]{2,1,0:T(8,128)}, bf16[16,256]{1,0:T(8,128)(2,1)}, bf16[16,256]{1,0:T(8,128)(2,1)}) custom-call(f32[4,16,320]{2,1,0:T(8,128)S(1)} %get-tuple-element.6.refs_0_, bf16[16,256]{1,0:T(8,128)(2,1)S(1)} %get-tuple-element.7.refs_1_, bf16[16,256]{1,0:T(8,128)(2,1)S(1)} %get-tuple-element.8.refs_2_), custom_call_target="tpu_custom_call" | custom-call | tf_op jit(solution)/shard_map/pallas_call | solution.py:830

commit v5 on v4

--- a/solution.py
+++ b/solution.py
@@ -171,14 +171,15 @@
         squares = jnp.concatenate(
             [squares, jnp.zeros((lanes - count, squares.shape[1]), jnp.float32)], axis=0
         )
-    ones = jnp.ones((8, squares.shape[1]), jnp.float32)
-    return lax.dot_general(
-        ones,
-        squares,
-        (((1,), (1,)), ((), ())),
-        precision=lax.Precision.HIGHEST,
-        preferred_element_type=jnp.float32,
-    )
+    pad = -squares.shape[1] % 128
+    if pad:
+        squares = jnp.concatenate(
+            [squares, jnp.zeros((squares.shape[0], pad), jnp.float32)], axis=1
+        )
+    folded = squares[:, :128]
+    for start in range(128, squares.shape[1], 128):
+        folded = folded + squares[:, start : start + 128]
+    return jnp.sum(jnp.transpose(folded), axis=0, keepdims=True)
 
 
 def kernel(
@@ -318,15 +319,18 @@
     def zpeer(tt):
         return (g, c, tt)
 
+    own_pair, far_pair = u * per, (1 - u) * per
     barrier = pltpu.get_barrier_semaphore()
-    for dg in range(n_grp):
-        for dc in range(n_ctx):
-            for dt in range(n_tp):
-                if dg + dc + dt > 0:
+    for tt in peers + [t]:
+        for dc in reversed(range(n_ctx)):
+            for core in (far_pair, own_pair):
+                for dk in reversed(range(per)):
+                    if tt is t and dc + dk == 0 and core is own_pair:
+                        continue
                     pl.semaphore_signal(
                         barrier,
                         inc=1,
-                        device_id=((g + dg) % n_grp, (c + dc) % n_ctx, (t + dt) % n_tp),
+                        device_id=(core + (k + dk) % per, (c + dc) % n_ctx, tt),
                         device_id_type=MESH,
                     )
 
@@ -365,7 +369,7 @@
     rows = jnp.concatenate(
         [state_ref[...].reshape(rows_count, width), clean_ref[...].astype(jnp.float32)], axis=0
     )
-    ssq_own[...] = row_squares(rows, lanes)[0:1]
+    ssq_own[...] = row_squares(rows, lanes)
 
     @pl.when(c == held)
     def _():
@@ -443,8 +447,8 @@
     def to_line(tt, device):
         link(h_buf.at[slot_of(k, tt), held], b_s.at[0], b_r.at[tt], device).start()
 
-    to_line(t, zpeer(across))
-    to_line(t, zpeer(pair))
+    for tt in (across, pair):
+        to_line(t, zpeer(tt))
     to_beside(held, t)
     to_sibling(held, t)
 
@@ -483,8 +487,8 @@
         tt = places[i]
         link(h_buf.at[slot_of(k, tt), u], n_s.at[0], n_r.at[tt], beside).wait_recv()
         if i in (0, 2):
-            device = zpeer(across if i == 0 else pair)
-            link(h_buf.at[slot_of(k, tt), u], n_s.at[0], n_r.at[tt], device).start()
+            place = across if i == 0 else pair
+            link(h_buf.at[slot_of(k, tt), u], n_s.at[0], n_r.at[tt], zpeer(place)).start()
         to_sibling(u, tt)
 
     def from_sibling(i):
@@ -499,19 +503,18 @@
     from_line(1)
     from_line(2)
     from_sibling(0)
-    add([slot_of(k, t), slot_of(1 - k, t)], True)
+    add([slot_of(k, places[0]), slot_of(1 - k, places[0])], True)
     from_beside(2)
     from_beside(1)
     from_line(3)
+    from_beside(3)
     from_sibling(1)
-    add([slot_of(k, pair), slot_of(1 - k, pair)])
-    from_beside(3)
     from_sibling(2)
-    add([slot_of(k, across), slot_of(1 - k, across), slot_of(k, diagonal)])
-    from_sibling(n_tp - 1)
+    add([slot_of(k, places[1]), slot_of(1 - k, places[1]), slot_of(k, places[2]), slot_of(1 - k, places[2]), slot_of(k, places[3])])
+    from_sibling(3)
     part_copies = []
     for w in range(3):
-        whole = acc[w] + project([slot_of(1 - k, diagonal)], w)
+        whole = acc[w] + project([slot_of(1 - k, places[3])], w)
         for head in range(n_ctx):
             piece = whole[:, head * HD : (head + 1) * HD]
             if w == 0:
@@ -672,7 +675,7 @@
     both_sources(cross_b, fb_s.at[0], xb_r.at[0])
     summed_b = cross_b[0].astype(jnp.float32) + cross_b[1].astype(jnp.float32)
     y_rows = jnp.concatenate([summed_a, summed_b], axis=0)
-    ssy_buf[0] = row_squares(y_rows, lanes)[0:1]
+    ssy_buf[0] = row_squares(y_rows, lanes)
     for d in range(1, members):
         remote(
             ssy_buf.at[0], ssy_buf.at[d], ssy_s.at[0], ssy_r.at[0], member((j + d) % members)

time: 47.1 us -> 46.4 us (0.985)
  Pallas kernels: 46.3 us -> 45.6 us
    pallas_call x1, Pallas kernels: 45.6 us -> 44.9 us  [fused(): pl.pallas_call(functools.partial(kernel, dims), out_shape=(pltpu.VMEM(sta...]
where the time goes in v5:
time: 46.4 us; the launch traced here: 46.3 us
  Pallas kernels  45.6 us (98%)
  between operations  0.64 us (1%)
    pallas_call x1, Pallas kernels, fused(): pl.pallas_call(functools.partial(kernel, dims), out_shape=(pltpu.VMEM(sta...  44.9 us

profile of v5, /device:TPU:0, one launch (start us, length us, event | category | flops | bytes accessed | tf_op | source)
XLA Modules:
  0.0 46.3 jit_solution(17340602968359144026)
XLA Ops:
  0.6 44.9 %shard_map.166 = (f32[4,16,320]{2,1,0:T(8,128)S(1)}, bf16[16,256]{1,0:T(8,128)(2,1)S(1)}, bf16[16,256]{1,0:T(8,128)(2,1)S(1)}) custom-call(f32[4,16,320]{2,1,0:T(8,128)} %state_hbm.1, bf16[16,320]{1,0:T(8,128)(2,1)} %clean_hbm.1, bf16[2560,256]{1,0:T(8,128)(2,1)} %wq_hbm.1, bf16[2560,256]{1,0:T(8,128)(2,1)} %wk_hbm.1, bf16[2560,256]{1,0:T(8,128)(2,1)} %wv_hbm.1, ...), custom_call_target="tpu_custom_call" | custom-call | tf_op jit(solution)/shard_map/pallas_call | solution.py:819
  45.6 0.7 %shard_map.167 = (f32[4,16,320]{2,1,0:T(8,128)}, bf16[16,256]{1,0:T(8,128)(2,1)}, bf16[16,256]{1,0:T(8,128)(2,1)}) custom-call(f32[4,16,320]{2,1,0:T(8,128)S(1)} %get-tuple-element.6.refs_0_, bf16[16,256]{1,0:T(8,128)(2,1)S(1)} %get-tuple-element.7.refs_1_, bf16[16,256]{1,0:T(8,128)(2,1)S(1)} %get-tuple-element.8.refs_2_), custom_call_target="tpu_custom_call" | custom-call | tf_op jit(solution)/shard_map/pallas_call | solution.py:833

commit v6 on v5

--- a/solution.py
+++ b/solution.py
@@ -244,37 +244,21 @@
     far_b,
     cross_b,
     local_sem,
-    cache_s,
+    send,
     cache_r,
-    ssq_s,
     ssq_r,
-    a_s,
     a_r,
-    b_s,
     b_r,
-    n_s,
     n_r,
-    c_s,
     c_r,
-    p_s,
     p_r,
-    f_s,
     f_r,
-    t_s,
     t_r,
-    wo_s,
     wo_r,
-    fa_s,
-    na_s,
     xa_r,
-    za_s,
     za_r,
-    zb_s,
     zb_r,
-    fb_s,
-    nb_s,
     xb_r,
-    ssy_s,
     ssy_r,
 ):
     n_grp, n_ctx, n_tp = dims
@@ -346,7 +330,7 @@
         for i, src in enumerate((ck_hbm, cv_hbm))
     ]
     small = [
-        pltpu.make_async_copy(src, dst, local_sem.at[3 + i])
+        pltpu.make_async_copy(src, dst, local_sem.at[3])
         for i, (src, dst) in enumerate(
             [
                 (state_hbm, state_ref),
@@ -391,7 +375,7 @@
     pl.semaphore_wait(barrier, n_grp * n_ctx * n_tp - 1)
 
     def ssq_copy(target):
-        return remote(ssq_own, ssq_buf.at[j], ssq_s.at[0], ssq_r.at[0], target)
+        return remote(ssq_own, ssq_buf.at[j], send.at[0], ssq_r.at[0], target)
 
     for dk in range(per):
         for dc in range(n_ctx):
@@ -403,13 +387,13 @@
                     copy.start()
                 else:
                     pl.when(c != held)(copy.start)
-    a_copy = remote(raw, raw_in, a_s.at[0], a_r.at[0], ((1 - c) * per + k, u, t))
+    a_copy = remote(raw, raw_in, send.at[0], a_r.at[0], ((1 - c) * per + k, u, t))
     a_copy.start()
     wo_load.wait()
     for block in range(per * n_tp):
         wo_cut[block] = wo_buf[:, block * width : (block + 1) * width]
     wo_copy = remote(
-        wo_cut.at[pl.ds((1 - k) * n_tp, n_tp)], wo_sib, wo_s.at[0], wo_r.at[0], sibling
+        wo_cut.at[pl.ds((1 - k) * n_tp, n_tp)], wo_sib, send.at[0], wo_r.at[0], sibling
     )
     wo_copy.start()
 
@@ -417,11 +401,11 @@
         @pl.when(c == held)
         def _():
             most = ssq_buf.at[: members - 1]
-            finish(remote(most, most, ssq_s.at[0], ssq_r.at[0], partner))
+            finish(remote(most, most, send.at[0], ssq_r.at[0], partner))
 
         @pl.when(c != held)
         def _():
-            finish(remote(ssq_buf, ssq_buf, ssq_s.at[0], ssq_r.at[0], partner))
+            finish(remote(ssq_buf, ssq_buf, send.at[0], ssq_r.at[0], partner))
 
     ssq_wait(lambda copy: copy.wait_recv())
     total = ssq_buf[0]
@@ -439,13 +423,13 @@
         return remote(ref, ref, send, recv, device)
 
     def to_beside(x, tt):
-        link(h_buf.at[slot_of(k, tt), x], n_s.at[0], n_r.at[tt], beside).start()
+        link(h_buf.at[slot_of(k, tt), x], send.at[0], n_r.at[tt], beside).start()
 
     def to_sibling(x, tt):
-        link(h_buf.at[slot_of(k, tt), x], c_s.at[0], c_r.at[tt], sibling).start()
+        link(h_buf.at[slot_of(k, tt), x], send.at[0], c_r.at[tt], sibling).start()
 
     def to_line(tt, device):
-        link(h_buf.at[slot_of(k, tt), held], b_s.at[0], b_r.at[tt], device).start()
+        link(h_buf.at[slot_of(k, tt), held], send.at[0], b_r.at[tt], device).start()
 
     for tt in (across, pair):
         to_line(t, zpeer(tt))
@@ -453,10 +437,10 @@
     to_sibling(held, t)
 
     cache_copies = [
-        remote(seen_buf.at[c], seen_buf.at[c], cache_s.at[0], cache_r.at[0], partner)
+        remote(seen_buf.at[c], seen_buf.at[c], send.at[0], cache_r.at[0], partner)
     ] + [
         remote(
-            src.at[:, other_lanes], cache_buf.at[c, i], cache_s.at[1], cache_r.at[1], partner
+            src.at[:, other_lanes], cache_buf.at[c, i], send.at[0], cache_r.at[1], partner
         )
         for i, src in enumerate((ck_hbm, cv_hbm))
     ]
@@ -476,7 +460,7 @@
 
     def from_line(i):
         tt = places[i]
-        link(h_buf.at[slot_of(k, tt), held], b_s.at[0], b_r.at[tt], partner).wait_recv()
+        link(h_buf.at[slot_of(k, tt), held], send.at[0], b_r.at[tt], partner).wait_recv()
         if i == 1:
             to_beside(held, tt)
         if i == 2:
@@ -485,15 +469,15 @@
 
     def from_beside(i):
         tt = places[i]
-        link(h_buf.at[slot_of(k, tt), u], n_s.at[0], n_r.at[tt], beside).wait_recv()
+        link(h_buf.at[slot_of(k, tt), u], send.at[0], n_r.at[tt], beside).wait_recv()
         if i in (0, 2):
             place = across if i == 0 else pair
-            link(h_buf.at[slot_of(k, tt), u], n_s.at[0], n_r.at[tt], zpeer(place)).start()
+            link(h_buf.at[slot_of(k, tt), u], send.at[0], n_r.at[tt], zpeer(place)).start()
         to_sibling(u, tt)
 
     def from_sibling(i):
         tt = places[i]
-        link(h_buf.at[slot_of(1 - k, tt)], c_s.at[0], c_r.at[tt], sibling).wait_recv()
+        link(h_buf.at[slot_of(1 - k, tt)], send.at[0], c_r.at[tt], sibling).wait_recv()
 
     def add(slots, fresh=False):
         for w in range(3):
@@ -526,17 +510,17 @@
                 kv_part[head, w - 1] = piece
                 kv_send[head, w - 1] = piece.astype(jnp.bfloat16)
         if w == 0:
-            copy = remote(q_part.at[other], q_in, p_s.at[0], p_r.at[0], partner)
+            copy = remote(q_part.at[other], q_in, send.at[0], p_r.at[0], partner)
         else:
             copy = remote(
-                kv_send.at[other, w - 1], kv_in.at[w - 1], p_s.at[1], p_r.at[w], partner
+                kv_send.at[other, w - 1], kv_in.at[w - 1], send.at[0], p_r.at[w], partner
             )
         copy.start()
         part_copies.append(copy)
     pltpu.make_async_copy(cache_buf.at[0], cache_buf.at[0], local_sem.at[2]).wait()
     cache_copies[0].wait_recv()
     both_caches = remote(
-        cache_buf.at[0], cache_buf.at[0], cache_s.at[1], cache_r.at[1], partner
+        cache_buf.at[0], cache_buf.at[0], send.at[0], cache_r.at[1], partner
     )
     both_caches.wait_recv()
     query_group = (lax.broadcasted_iota(jnp.int32, (queries, total_rows), 0) % rows_count) // ch
@@ -582,20 +566,20 @@
     attention = (numer / denom).astype(jnp.bfloat16)
     att_buf[k * n_ctx + c] = attention
     for device in (partner, (u * per + (1 - k), other, t), sibling):
-        link(att_buf.at[k * n_ctx + c], t_s.at[0], t_r.at[0], device).start()
+        link(att_buf.at[k * n_ctx + c], send.at[0], t_r.at[0], device).start()
 
     for x in range(n_ctx):
         last = slice(x * all_rows + rows_count, (x + 1) * all_rows)
         kv_buf[x, 0] = key[last]
         kv_buf[x, 1] = value[last]
-    fin_copy = remote(kv_buf.at[other], fin_in, f_s.at[0], f_r.at[0], partner)
+    fin_copy = remote(kv_buf.at[other], fin_in, send.at[0], f_r.at[0], partner)
     fin_copy.start()
     nk_ref[:, own_lanes] = kv_buf[c, 0]
     nv_ref[:, own_lanes] = kv_buf[c, 1]
 
     wo_copy.wait_recv()
     shared = att_buf.at[: per * n_ctx - 1]
-    att_all = link(shared, t_s.at[0], t_r.at[0], partner)
+    att_all = link(shared, send.at[0], t_r.at[0], partner)
     att_all.wait_recv()
     order = peers + [t]
 
@@ -613,15 +597,15 @@
             return y_part[i, at, :]
 
         far_a[i] = chunk(other, 0, first).astype(jnp.bfloat16)
-        remote(far_a.at[i], cross_a.at[tt, u], fa_s.at[0], xa_r.at[tt], owner).start()
+        remote(far_a.at[i], cross_a.at[tt, u], send.at[0], xa_r.at[tt], owner).start()
         near_a[i] = chunk(c, 0, first).astype(jnp.bfloat16)
-        near = remote(near_a.at[i], cross_a.at[tt, u], na_s.at[0], xa_r.at[tt], beside)
+        near = remote(near_a.at[i], cross_a.at[tt, u], send.at[0], xa_r.at[tt], beside)
         pl.when(jnp.logical_not(at_home))(near.start)
 
         if i < n_tp - 1:
             for x in range(n_ctx):
                 zb_send[i, x] = chunk(x, first, late).astype(jnp.bfloat16)
-            remote(zb_send.at[i], zb_in.at[t], zb_s.at[0], zb_r.at[0], zpeer(tt)).start()
+            remote(zb_send.at[i], zb_in.at[t], send.at[0], zb_r.at[0], zpeer(tt)).start()
 
     fin_copy.wait_recv()
     nk_ref[:, other_lanes] = fin_in[0]
@@ -636,19 +620,21 @@
         def _():
             remote(ref, ref, send, recv, partner).wait_recv()
 
-    for i, tt in enumerate(order):
+    def from_across(i):
+        tt = order[i]
 
         @pl.when(at_home)
         def _():
             cross_a[tt, u] = near_a[i]
 
-        both_sources(cross_a.at[tt], fa_s.at[0], xa_r.at[tt])
-        summed_a = cross_a[tt, 0].astype(jnp.float32) + cross_a[tt, 1].astype(jnp.float32)
-        if i < n_tp - 1:
-            za_send[i] = summed_a.astype(jnp.bfloat16)
-            remote(za_send.at[i], za_in.at[t], za_s.at[0], za_r.at[0], zpeer(tt)).start()
-
-    link(zb_send, zb_s.at[0], zb_r.at[0], partner).wait_recv()
+        both_sources(cross_a.at[tt], send.at[0], xa_r.at[tt])
+        return cross_a[tt, 0].astype(jnp.float32) + cross_a[tt, 1].astype(jnp.float32)
+
+    for i in range(n_tp - 1):
+        za_send[i] = from_across(i).astype(jnp.bfloat16)
+        remote(za_send.at[i], za_in.at[t], send.at[0], za_r.at[0], zpeer(order[i])).start()
+
+    link(zb_send, send.at[0], zb_r.at[0], partner).wait_recv()
 
     def gathered(x):
         at = pl.ds(pl.multiple_of(x * rows_count + first, ch), late)
@@ -658,13 +644,14 @@
         return result.astype(jnp.bfloat16)
 
     far_b[...] = gathered(other)
-    far_copy = remote(far_b, cross_b.at[u], fb_s.at[0], xb_r.at[0], owner)
+    far_copy = remote(far_b, cross_b.at[u], send.at[0], xb_r.at[0], owner)
     far_copy.start()
     near_b[...] = gathered(c)
-    near_copy = remote(near_b, cross_b.at[u], nb_s.at[0], xb_r.at[0], beside)
+    near_copy = remote(near_b, cross_b.at[u], send.at[0], xb_r.at[0], beside)
     pl.when(jnp.logical_not(at_home))(near_copy.start)
 
-    link(za_send, za_s.at[0], za_r.at[0], partner).wait_recv()
+    summed_a = from_across(n_tp - 1)
+    link(za_send, send.at[0], za_r.at[0], partner).wait_recv()
     for tt in peers:
         summed_a = summed_a + za_in[tt].astype(jnp.float32)
 
@@ -672,25 +659,25 @@
     def _():
         cross_b[u] = near_b[...]
 
-    both_sources(cross_b, fb_s.at[0], xb_r.at[0])
+    both_sources(cross_b, send.at[0], xb_r.at[0])
     summed_b = cross_b[0].astype(jnp.float32) + cross_b[1].astype(jnp.float32)
     y_rows = jnp.concatenate([summed_a, summed_b], axis=0)
     ssy_buf[0] = row_squares(y_rows, lanes)
     for d in range(1, members):
         remote(
-            ssy_buf.at[0], ssy_buf.at[d], ssy_s.at[0], ssy_r.at[0], member((j + d) % members)
+            ssy_buf.at[0], ssy_buf.at[d], send.at[0], ssy_r.at[0], member((j + d) % members)
         ).start()
     ssq_wait(lambda copy: copy.wait_send())
     slots = n_tp - 1
-    for ref, send in (
-        (h_buf.at[:slots, 0], b_s),
-        (h_buf.at[: n_tp // n_ctx], n_s),
-        (h_buf.at[:n_tp], c_s),
-        (kv_send.at[0], p_s.at[1:]),
-        (shared, t_s),
-        (far_a, fa_s),
-        (za_send, za_s),
-        (zb_send, zb_s),
+    for ref in (
+        h_buf.at[:slots, 0],
+        h_buf.at[: n_tp // n_ctx],
+        h_buf.at[:n_tp],
+        kv_send.at[0],
+        shared,
+        far_a,
+        za_send,
+        zb_send,
     ):
         link(ref, send.at[0], send.at[0], partner).wait_send()
     for copy in [a_copy, cache_copies[0], both_caches, part_copies[0], wo_copy, fin_copy, far_copy]:
@@ -698,11 +685,11 @@
 
     @pl.when(jnp.logical_not(at_home))
     def _():
-        link(near_a, na_s.at[0], na_s.at[0], partner).wait_send()
+        link(near_a, send.at[0], send.at[0], partner).wait_send()
         near_copy.wait_send()
 
     rest = ssy_buf.at[1:]
-    ssy_all = remote(rest, rest, ssy_s.at[0], ssy_r.at[0], partner)
+    ssy_all = remote(rest, rest, send.at[0], ssy_r.at[0], partner)
     ssy_all.wait_recv()
     total = ssy_buf[0]
     for d in range(1, members):
@@ -748,9 +735,6 @@
     dma = pltpu.SemaphoreType.DMA
     vm = pl.BlockSpec(memory_space=pltpu.VMEM)
     hbm = pl.BlockSpec(memory_space=pltpu.HBM)
-
-    def pair(count):
-        return [dma((count,))] * 2
 
     scratch = [
         pltpu.VMEM(state.shape, fl),
@@ -791,30 +775,23 @@
         pltpu.VMEM((late, width), bf),
         pltpu.VMEM((late, width), bf),
         pltpu.VMEM((n_ctx, late, width), bf),
-        dma((12,)),
-        *pair(2),
-        *pair(1),
-        *pair(1),
+        dma((4,)),
+        dma((1,)),
+        dma((2,)),
+        dma((1,)),
         dma((1,)),
         dma((n_tp,)),
-        dma((1,)),
         dma((n_tp,)),
-        dma((1,)),
         dma((n_tp,)),
-        dma((2,)),
         dma((3,)),
-        *pair(1),
-        *pair(1),
-        *pair(1),
+        dma((1,)),
         dma((1,)),
         dma((1,)),
         dma((n_tp,)),
-        *pair(1),
-        *pair(1),
-        dma((1,)),
-        dma((1,)),
-        dma((1,)),
-        *pair(1),
+        dma((1,)),
+        dma((1,)),
+        dma((1,)),
+        dma((1,)),
     ]
     results = pl.pallas_call(
         functools.partial(kernel, dims),

time: 46.4 us -> 45.8 us (0.987)
  Pallas kernels: 45.6 us -> 45 us
    pallas_call x1, Pallas kernels: 44.9 us -> 44.3 us  [fused(): pl.pallas_call(functools.partial(kernel, dims), out_shape=(pltpu.VMEM(sta...]
where the time goes in v6:
time: 45.8 us; the launch traced here: 45.6 us
  Pallas kernels  45 us (98%)
  between operations  0.64 us (1%)
    pallas_call x1, Pallas kernels, fused(): pl.pallas_call(functools.partial(kernel, dims), out_shape=(pltpu.VMEM(sta...  44.3 us

profile of v6, /device:TPU:0, one launch (start us, length us, event | category | flops | bytes accessed | tf_op | source)
XLA Modules:
  0.0 45.6 jit_solution(11145722536605519125)
XLA Ops:
  0.6 44.3 %shard_map.166 = (f32[4,16,320]{2,1,0:T(8,128)S(1)}, bf16[16,256]{1,0:T(8,128)(2,1)S(1)}, bf16[16,256]{1,0:T(8,128)(2,1)S(1)}) custom-call(f32[4,16,320]{2,1,0:T(8,128)} %state_hbm.1, bf16[16,320]{1,0:T(8,128)(2,1)} %clean_hbm.1, bf16[2560,256]{1,0:T(8,128)(2,1)} %wq_hbm.1, bf16[2560,256]{1,0:T(8,128)(2,1)} %wk_hbm.1, bf16[2560,256]{1,0:T(8,128)(2,1)} %wv_hbm.1, ...), custom_call_target="tpu_custom_call" | custom-call | tf_op jit(solution)/shard_map/pallas_call | solution.py:796
  45.0 0.7 %shard_map.167 = (f32[4,16,320]{2,1,0:T(8,128)}, bf16[16,256]{1,0:T(8,128)(2,1)}, bf16[16,256]{1,0:T(8,128)(2,1)}) custom-call(f32[4,16,320]{2,1,0:T(8,128)S(1)} %get-tuple-element.6.refs_0_, bf16[16,256]{1,0:T(8,128)(2,1)S(1)} %get-tuple-element.7.refs_1_, bf16[16,256]{1,0:T(8,128)(2,1)S(1)} %get-tuple-element.8.refs_2_), custom_call_target="tpu_custom_call" | custom-call | tf_op jit(solution)/shard_map/pallas_call | solution.py:810

commit v7 on v6

--- a/solution.py
+++ b/solution.py
@@ -431,10 +431,10 @@
     def to_line(tt, device):
         link(h_buf.at[slot_of(k, tt), held], send.at[0], b_r.at[tt], device).start()
 
+    to_beside(held, t)
+    to_sibling(held, t)
     for tt in (across, pair):
         to_line(t, zpeer(tt))
-    to_beside(held, t)
-    to_sibling(held, t)
 
     cache_copies = [
         remote(seen_buf.at[c], seen_buf.at[c], send.at[0], cache_r.at[0], partner)
@@ -484,8 +484,8 @@
             acc[w] = project(slots, w) if fresh else acc[w] + project(slots, w)
 
     from_beside(0)
+    from_line(2)
     from_line(1)
-    from_line(2)
     from_sibling(0)
     add([slot_of(k, places[0]), slot_of(1 - k, places[0])], True)
     from_beside(2)
@@ -688,6 +688,12 @@
         link(near_a, send.at[0], send.at[0], partner).wait_send()
         near_copy.wait_send()
 
+    gained = y_rows * og_ref[...].reshape(1, width)
+    moves = []
+    for f in range(flight):
+        now = levels_ref[noise_ref[f]]
+        after = levels_ref[noise_ref[f] + 1]
+        moves.append((after - now) * gained[f * ch : (f + 1) * ch])
     rest = ssy_buf.at[1:]
     ssy_all = remote(rest, rest, send.at[0], ssy_r.at[0], partner)
     ssy_all.wait_recv()
@@ -695,11 +701,8 @@
     for d in range(1, members):
         total = total + ssy_buf[d]
     inverse = lax.rsqrt(jnp.transpose(jnp.broadcast_to(total, (8, lanes)))[:rows_count, 0:1] / D + epsilon)
-    velocity = y_rows * inverse * og_ref[...].reshape(1, width)
     for f in range(flight):
-        now = levels_ref[noise_ref[f]]
-        after = levels_ref[noise_ref[f] + 1]
-        out_ref[f] = state_ref[f] + (after - now) * velocity[f * ch : (f + 1) * ch]
+        out_ref[f] = state_ref[f] + moves[f] * inverse[f * ch : (f + 1) * ch]
     ssy_all.wait_send()
 
 

time: 45.8 us -> 45.8 us (level)
  no operation moved by 1% of the time
where the time goes in v7:
time: 45.8 us; the launch traced here: 45.7 us
  Pallas kernels  45 us (98%)
  between operations  0.64 us (1%)
    pallas_call x1, Pallas kernels, fused(): pl.pallas_call(functools.partial(kernel, dims), out_shape=(pltpu.VMEM(sta...  44.3 us

profile of v7, /device:TPU:0, one launch (start us, length us, event | category | flops | bytes accessed | tf_op | source)
XLA Modules:
  0.0 45.7 jit_solution(6316680255456729045)
XLA Ops:
  0.6 44.3 %shard_map.166 = (f32[4,16,320]{2,1,0:T(8,128)S(1)}, bf16[16,256]{1,0:T(8,128)(2,1)S(1)}, bf16[16,256]{1,0:T(8,128)(2,1)S(1)}) custom-call(f32[4,16,320]{2,1,0:T(8,128)} %state_hbm.1, bf16[16,320]{1,0:T(8,128)(2,1)} %clean_hbm.1, bf16[2560,256]{1,0:T(8,128)(2,1)} %wq_hbm.1, bf16[2560,256]{1,0:T(8,128)(2,1)} %wk_hbm.1, bf16[2560,256]{1,0:T(8,128)(2,1)} %wv_hbm.1, ...), custom_call_target="tpu_custom_call" | custom-call | tf_op jit(solution)/shard_map/pallas_call | solution.py:799
  45.0 0.7 %shard_map.167 = (f32[4,16,320]{2,1,0:T(8,128)}, bf16[16,256]{1,0:T(8,128)(2,1)}, bf16[16,256]{1,0:T(8,128)(2,1)}) custom-call(f32[4,16,320]{2,1,0:T(8,128)S(1)} %get-tuple-element.6.refs_0_, bf16[16,256]{1,0:T(8,128)(2,1)S(1)} %get-tuple-element.7.refs_1_, bf16[16,256]{1,0:T(8,128)(2,1)S(1)} %get-tuple-element.8.refs_2_), custom_call_target="tpu_custom_call" | custom-call | tf_op jit(solution)/shard_map/pallas_call | solution.py:813
